TPU v7x, 256 devices: a whole 4x4x8 slice. The times are simulated.
256 devices in a mesh: pipe: 4 (over y_lo, core), ctx: 16 (over z, y_hi), tp: 4 (over x).
Axes of the slice: x: 4, y: 4 (y_hi: 2, y_lo: 2; y = y_hi * 2 + y_lo), z: 8, core: 2. Of those that a mesh axis runs over, the one named last changes fastest.
Arguments:
- segment_inputs: bfloat16 [4, 2, 2048, 4096], P('pipe', None, ('ctx', 'tp')), may hold values from -128 to 128
- keys: bfloat16 [4, 2, 2048, 512], P('pipe', None, 'ctx', 'tp'), may hold values from -64 to 64
- values: bfloat16 [4, 2, 2048, 512], P('pipe', None, 'ctx', 'tp'), may hold values from -6 to 6
- norm_gain: float32 [4, 4096], P('pipe'), may hold values from 0.1 to 1.9
- waiting_grads: bfloat16 [4, 2048, 4096], P('pipe', ('ctx', 'tp')), may hold values from -32 to 32
- output_grads: bfloat16 [1, 2048, 4096], P(None, ('ctx', 'tp')), may hold values from -32 to 32
- doc_lengths: int32 [5, 8], replicated, may hold values from 1 to 1024, as said below
Outputs:
- input_grads: bfloat16 [4, 2, 2048, 4096], P('pipe', None, ('ctx', 'tp'))
- key_grads: float32 [4, 2, 2048, 512], P('pipe', None, 'ctx', 'tp')
- value_grads: float32 [4, 2, 2048, 512], P('pipe', None, 'ctx', 'tp')
- gain_grads: float32 [4, 4096], P('pipe')
Inputs may be any that keep to these rules, and one draw needn't show every extreme that they name: `doc_lengths`: row m lists in order of position the lengths of the 8 documents packed into microbatch m's sequence; each row sums to 2048; the last document is exactly 1024 long.
All inputs are finite; a program needn't handle non-finite values.
Results may differ from a plain program's by a relative error of at most 0.009.
The roundings to bfloat16 on the way count: a program that leaves them out, or rounds other values in their place, can miss the bound.
Values may be sent and summed in bfloat16 or wider, within the bound.
A program may use at most 64 MiB of HBM per device.

v0:
```python
import jax
import jax.numpy as jnp
from jax import lax
from jax.sharding import PartitionSpec as P

HD = 128
S_DEV = 128
TICKS = 2


epsilon = 1e-05
masked_fill = -1e30


def passed_along(value, axis, by):
    count = lax.axis_size(axis)
    return lax.ppermute(value, axis, [(i, (i + by) % count) for i in range(count)])


def from_behind(value, axis, steps):
    count = lax.axis_size(axis)
    first, last = (max(0, -steps), min(count, count - steps))
    return lax.ppermute(value, axis, [(source, source + steps) for source in range(first, last)])


def row_positions(rows, half_rows, cycle_count):
    section = rows // half_rows
    offset = rows % half_rows
    owner = section // 2
    placed = jnp.where(section % 2 == 0, owner, 2 * cycle_count - 1 - owner)
    return placed * half_rows + offset


def document_starts(lengths_row, positions):
    closing = jnp.cumsum(lengths_row)
    passed = closing[None, :] <= positions[:, None]
    return jnp.sum(jnp.where(passed, lengths_row[None, :], 0), axis=1)


def keep_same(current):
    return current


def key_positions(key_first, key_count, cycle_count):
    rows = key_first + jnp.arange(key_count, dtype=jnp.int32)
    return row_positions(rows, S_DEV // 2, cycle_count)


def block_active(key_first, key_count, query_pos, query_start, cycle_count):
    key_pos = key_positions(key_first, key_count, cycle_count)
    return (jnp.min(key_pos) <= jnp.max(query_pos)) & (jnp.max(key_pos) >= jnp.min(query_start))


def score_block(query_block, key_block, query_pos, query_start, key_first, cycle_count):
    key_count = key_block.shape[0]
    key_pos = key_positions(key_first, key_count, cycle_count)
    scores = HD ** (-0.5) * jnp.einsum(
        "rkgd,skd->kgrs", query_block, key_block, preferred_element_type=jnp.float32
    )
    visible = (key_pos[None, :] <= query_pos[:, None]) & (key_pos[None, :] >= query_start[:, None])
    return (scores, visible[None, None])


def forward_update(carry, key_flat, value_flat, key_first, context):
    query_block, grad_block, query_pos, query_start, cycle_count = context
    key_count = key_flat.shape[0]

    def apply_block(current):
        row_peak, row_total, weighted = current
        key_block = key_flat.reshape(key_count, -1, HD)
        value_block = value_flat.reshape(key_count, -1, HD)
        scores, visible = score_block(
            query_block, key_block, query_pos, query_start, key_first, cycle_count
        )
        block_peak = jnp.max(jnp.where(visible, scores, masked_fill), axis=-1)
        new_peak = jnp.maximum(row_peak, block_peak)
        weights = jnp.where(visible, jnp.exp(scores - new_peak[..., None]), 0.0)
        prob_grad = jnp.einsum(
            "rkgd,skd->kgrs", grad_block, value_block, preferred_element_type=jnp.float32
        )
        return (new_peak, jnp.sum(weights, axis=-1), jnp.sum(weights * prob_grad, axis=-1))

    return lax.cond(
        block_active(key_first, key_count, query_pos, query_start, cycle_count),
        apply_block,
        keep_same,
        carry,
    )


def backward_terms(key_flat, value_flat, key_first, context, row_stats):
    query_block, grad_block, query_pos, query_start, cycle_count = context
    logsum, row_term = row_stats
    key_count = key_flat.shape[0]
    key_block = key_flat.reshape(key_count, -1, HD)
    value_block = value_flat.reshape(key_count, -1, HD)
    scale_factor = HD ** (-0.5)
    scores, visible = score_block(
        query_block, key_block, query_pos, query_start, key_first, cycle_count
    )
    prob_weights = jnp.where(visible, jnp.exp(scores - logsum[..., None]), 0.0)
    prob_grad = jnp.einsum(
        "rkgd,skd->kgrs", grad_block, value_block, preferred_element_type=jnp.float32
    )
    dscore = (prob_weights * (prob_grad - row_term[..., None])).astype(jnp.bfloat16)
    probs_low = prob_weights.astype(jnp.bfloat16)
    query_add = scale_factor * jnp.einsum(
        "kgrs,skd->rkgd", dscore, key_block, preferred_element_type=jnp.float32
    )
    key_add = scale_factor * jnp.einsum(
        "kgrs,rkgd->skd", dscore, query_block, preferred_element_type=jnp.float32
    )
    value_add = jnp.einsum(
        "kgrs,rkgd->skd", probs_low, grad_block, preferred_element_type=jnp.float32
    )
    return (query_add, key_add.reshape(key_count, -1), value_add.reshape(key_count, -1))


def segment_tick(inputs, key_local, value_local, gain_row, arriving, lengths_row):
    widened = inputs.astype(jnp.float32)
    inverse = lax.rsqrt(jnp.mean(widened * widened, axis=-1, keepdims=True) + epsilon)
    normed = widened * inverse
    queries = (normed * gain_row[None, :]).astype(jnp.bfloat16)
    query_heads, grad_heads = (
        lax.all_to_all(queries, "tp", split_axis=1, concat_axis=0, tiled=True),
        lax.all_to_all(arriving, "tp", split_axis=1, concat_axis=0, tiled=True),
    )
    row_count = key_local.shape[0]
    kv_local = key_local.shape[1] // HD
    group_size = query_heads.shape[1] // (HD * kv_local)
    query_block = query_heads.reshape(row_count, kv_local, group_size, HD)
    grad_block = grad_heads.reshape(row_count, kv_local, group_size, HD)
    cycle_count = lax.axis_size("ctx")
    cycle_place = lax.axis_index("ctx")
    query_pos = key_positions(cycle_place * row_count, row_count, cycle_count)
    query_start = document_starts(lengths_row, query_pos)
    context = (query_block, grad_block, query_pos, query_start, cycle_count)
    empty_peak = jnp.full((kv_local, group_size, row_count), masked_fill, jnp.float32)
    zero_rows = jnp.zeros((kv_local, group_size, row_count), jnp.float32)
    initial = (empty_peak, zero_rows, zero_rows)
    row_peak, row_total, weighted = forward_update(
        initial,
        lax.all_gather(key_local, "ctx", axis=0, tiled=True),
        lax.all_gather(value_local, "ctx", axis=0, tiled=True),
        jnp.int32(0),
        context,
    )
    row_stats = (row_peak + jnp.log(row_total), weighted / row_total)
    query_zero = jnp.zeros((row_count, kv_local, group_size, HD), jnp.float32)

    def cycle_turn(cycle_step, carry):
        key_block, value_block, key_grad, value_grad, query_grad = carry
        owner_index = (cycle_place - cycle_step) % cycle_count
        block_first = owner_index * row_count

        def apply_terms(current):
            added_terms = backward_terms(key_block, value_block, block_first, context, row_stats)
            return (
                current[0] + added_terms[1],
                current[1] + added_terms[2],
                current[2] + added_terms[0],
            )

        key_grad, value_grad, query_grad = lax.cond(
            block_active(block_first, row_count, query_pos, query_start, cycle_count),
            apply_terms,
            keep_same,
            (key_grad, value_grad, query_grad),
        )
        key_block, value_block = passed_along((key_block, value_block), "ctx", 1)
        key_grad, value_grad = passed_along((key_grad, value_grad), "ctx", 1)
        return (key_block, value_block, key_grad, value_grad, query_grad)

    zero_kv = jnp.zeros(key_local.shape, jnp.float32)
    finished = lax.fori_loop(
        0, cycle_count, cycle_turn, (key_local, value_local, zero_kv, zero_kv, query_zero)
    )
    key_grad, value_grad, query_grad = (finished[2], finished[3], finished[4])
    query_low = query_grad.reshape(row_count, -1).astype(jnp.bfloat16)
    grad_rows = lax.all_to_all(query_low, "tp", split_axis=0, concat_axis=1, tiled=True)
    rounded = grad_rows.astype(jnp.float32)
    scaled = rounded * gain_row[None, :]
    coupling = jnp.mean(scaled * normed, axis=-1, keepdims=True)
    input_grad = (arriving.astype(jnp.float32) + inverse * (scaled - normed * coupling)).astype(
        jnp.bfloat16
    )
    gain_part = jnp.sum(rounded * normed, axis=0)
    return (input_grad, key_grad, value_grad, gain_part)


def on_device(segment_inputs, keys, values, norm_gain, waiting_grads, output_grads, doc_lengths):
    segment_index = lax.axis_index("pipe")
    last_segment = lax.axis_size("pipe") - 1
    gain_row = norm_gain[0]
    arriving = waiting_grads[0]
    input_list = []
    key_list = []
    value_list = []
    gain_running = jnp.zeros(gain_row.shape, jnp.float32)
    for tick_index in range(TICKS):
        micro_index = segment_index + tick_index
        lengths_row = lax.dynamic_index_in_dim(doc_lengths, micro_index, 0, keepdims=False)
        input_grad, key_grad, value_grad, gain_part = segment_tick(
            segment_inputs[0, tick_index],
            keys[0, tick_index],
            values[0, tick_index],
            gain_row,
            arriving,
            lengths_row,
        )
        input_list.append(input_grad)
        key_list.append(key_grad)
        value_list.append(value_grad)
        gain_running = gain_running + gain_part
        if tick_index + 1 < TICKS:
            arrived = from_behind(input_grad, "pipe", -1)
            arriving = jnp.where(segment_index == last_segment, output_grads[tick_index], arrived)
    gain_grads = lax.psum(gain_running, ("ctx", "tp"))
    return (
        jnp.stack(input_list)[None],
        jnp.stack(key_list)[None],
        jnp.stack(value_list)[None],
        gain_grads[None],
    )


def solution(mesh):
    in_specs = (
        P("pipe", None, ("ctx", "tp"), None),
        P("pipe", None, "ctx", "tp"),
        P("pipe", None, "ctx", "tp"),
        P("pipe", None),
        P("pipe", ("ctx", "tp"), None),
        P(None, ("ctx", "tp"), None),
        P(),
    )
    out_specs = (
        P("pipe", None, ("ctx", "tp"), None),
        P("pipe", None, "ctx", "tp"),
        P("pipe", None, "ctx", "tp"),
        P("pipe", None),
    )
    return jax.shard_map(
        on_device, mesh=mesh, in_specs=in_specs, out_specs=out_specs, check_vma=False
    )
```

profile of v0, /device:TPU:8, one launch (start us, length us, event | category | flops | bytes accessed | tf_op | source)
XLA Modules:
  0.0 1165.9 jit_solution(12238675916187327474)
XLA Ops:
  6.3 4.3 all-to-all-start
  21.4 46.2 %all-gather = bf16[1,1,2048,128]{3,2,1,0:T(8,128)(2,1)S(1)} all-gather(bf16[1,1,128,128]{3,2,1,0:T(8,128)(2,1)S(1)} %get-tuple-element.1508), channel_id=2, replica_groups=mesh['pipe'=4,'ctx'=16,'tp'=4] {'ctx'}, dimensions={2}, use_global_device_ids=true | all-gather | bytes 557056 | tf_op jit(solution)/shard_map/all_gather | solution.py:143
  67.7 4.5 all-to-all-start.1
  72.2 40.6 %all-gather.1 = bf16[1,1,2048,128]{3,2,1,0:T(8,128)(2,1)} all-gather(bf16[1,1,128,128]{3,2,1,0:T(8,128)(2,1)S(1)} %get-tuple-element.1495), channel_id=3, replica_groups=mesh['pipe'=4,'ctx'=16,'tp'=4] {'ctx'}, dimensions={2}, use_global_device_ids=true | all-gather | bytes 557056 | tf_op jit(solution)/shard_map/all_gather | solution.py:144
  113.0 6.8 conditional.4
  120.0 273.9 %while.50 = (s32[]{:T(128)}, bf16[128,128]{1,0:T(8,128)(2,1)S(1)}, bf16[128,128]{1,0:T(8,128)(2,1)S(1)}, f32[128,128]{1,0:T(8,128)S(1)}, f32[128,128]{1,0:T(8,12...) while((s32[]{:T(128)}, bf16[128,128]{1,0:T(8,128)(2,1)S(1)}, ...), condition=%wide.region_17.18_spmd.clone, body=%wide.region_12.17_spmd.clone.sunk | while | flops 169071120 | bytes 6050608 | solution.py:175
  145.4 4.3 collective-permute-start.1
  211.9 4.9 collective-permute-start.3
  219.8 4.8 collective-permute-done
  249.4 4.5 collective-permute-start.1
  282.3 4.7 collective-permute-start.1
  347.7 4.5 collective-permute-start.3
  355.6 4.1 collective-permute-done
  381.0 4.3 collective-permute-start.3
  386.3 4.7 collective-permute-start.1
  394.9 5.4 all-to-all-start.2
  400.3 6.7 all-to-all-done.2
  411.5 41.4 %all-gather.2 = bf16[1,1,2048,128]{3,2,1,0:T(8,128)(2,1)S(1)} all-gather(bf16[1,1,128,128]{3,2,1,0:T(8,128)(2,1)S(1)} %get-tuple-element.1505), channel_id=4, replica_groups=mesh['pipe'=4,'ctx'=16,'tp'=4] {'ctx'}, dimensions={2}, use_global_device_ids=true | all-gather | bytes 557056 | tf_op jit(solution)/shard_map/all_gather | solution.py:143
  454.9 41.8 %all-gather.3 = bf16[1,1,2048,128]{3,2,1,0:T(8,128)(2,1)} all-gather(bf16[1,1,128,128]{3,2,1,0:T(8,128)(2,1)S(1)} %get-tuple-element.1492), channel_id=5, replica_groups=mesh['pipe'=4,'ctx'=16,'tp'=4] {'ctx'}, dimensions={2}, use_global_device_ids=true | all-gather | bytes 557056 | tf_op jit(solution)/shard_map/all_gather | solution.py:144
  502.7 4.1 all-to-all-done.3
  512.4 5.1 all-to-all-done.4
  518.6 6.9 conditional.5
  525.6 273.6 %while.51 = (s32[]{:T(128)}, bf16[128,128]{1,0:T(8,128)(2,1)S(1)}, bf16[128,128]{1,0:T(8,128)(2,1)S(1)}, f32[128,128]{1,0:T(8,128)S(1)}, f32[128,128]{1,0:T(8,12...) while((s32[]{:T(128)}, bf16[128,128]{1,0:T(8,128)(2,1)S(1)}, ...), condition=%wide.region_33.34_spmd.clone, body=%wide.region_28.33_spmd.clone.sunk | while | flops 169071120 | bytes 6050608 | solution.py:175
  550.4 4.7 collective-permute-start.5
  616.8 4.9 collective-permute-start.7
  624.7 4.5 collective-permute-done.4
  655.0 4.7 collective-permute-start.5
  753.7 4.9 collective-permute-start.7
  761.6 4.5 collective-permute-done.4
  791.7 4.7 collective-permute-start.5
  805.0 5.3 all-to-all-done.5
  810.8 353.9 %psum.7 = f32[1,4096]{1,0:T(1,128)} all-reduce(f32[1,4096]{1,0:T(1,128)S(1)} %bitcast.426), channel_id=1, replica_groups=mesh['pipe'=4,'ctx'=16,'tp'=4] {'ctx','tp'}, use_global_device_ids=true, to_apply=%region_37.38 | all-reduce | flops 4096 | bytes 32768 | tf_op jit(solution)/shard_map/psum | solution.py:218
  (988 shorter events, 487.4 us)
Async XLA Ops:
  6.3 61.3 %all-to-all-start = ((bf16[32,4,1024]{2,0,1:T(8,128)(2,1)}), bf16[32,4,1024]{2,0,1:T(8,128)(2,1)S(1)}, u32[]{:S(2)}, u32[]{:S(2)}) async-start(bf16[32,4,1024]{2,0,1:T(8,128)(2,1)} %multiply_convert_fusion.1), calls=%async_computation | async-start | bytes 524288 | tf_op jit(solution)/shard_map/all_to_all | solution.py:125
  67.7 45.2 %all-to-all-start.1 = ((bf16[32,4,1024]{2,0,1:T(8,128)(2,1)}), bf16[32,4,1024]{2,0,1:T(8,128)(2,1)S(1)}, u32[]{:S(2)}, u32[]{:S(2)}) async-start(bf16[32,4,1024]{2,0,1:T(8,128)(2,1)} %copy.84), calls=%async_computation.1 | async-start | bytes 524288 | tf_op jit(solution)/shard_map/all_to_all | solution.py:126
  143.1 9.3 collective-permute-start.3
  157.8 9.0 collective-permute-start.2
  177.8 8.6 collective-permute-start.3
  192.7 8.8 collective-permute-start.2
  192.8 8.7 collective-permute-start.3
  229.7 8.7 collective-permute-start.3
  245.0 9.0 collective-permute-start.2
  245.1 8.9 collective-permute-start.3
  279.8 8.6 collective-permute-start.2
  279.8 9.8 collective-permute-start.3
  295.0 10.4 collective-permute-start.2
  346.5 9.0 collective-permute-start.2
  380.8 10.3 collective-permute-start.2
  381.0 10.1 collective-permute-start.3
  394.9 12.0 %all-to-all-start.2 = ((bf16[4,32,1024]{2,1,0:T(8,128)(2,1)}), bf16[4,32,1024]{2,1,0:T(8,128)(2,1)S(1)}, u32[]{:S(2)}, u32[]{:S(2)}) async-start(bf16[4,32,1024]{2,1,0:T(8,128)(2,1)} %convert_element_type.172), calls=%async_computation.2 | async-start | bytes 524288 | tf_op jit(solution)/shard_map/all_to_all | solution.py:180
  409.6 91.3 %collective-permute-start.8 = (bf16[32,4096]{1,0:T(8,128)(2,1)}, bf16[32,4096]{1,0:T(8,128)(2,1)}, u32[]{:S(2)}, u32[]{:S(2)}) collective-permute-start(bf16[32,4096]{1,0:T(8,128)(2,1)} %fusion.122), channel_id=1, source_target_pairs={{64,0},{128,64},{192,128},{65,1},{129,65},{193,129},{66,2},{130,66... | collective-permute-start | bytes 786440 | tf_op jit(solution)/shard_map/ppermute | solution.py:23
  496.7 10.1 all-to-all-start.3
  506.8 10.8 all-to-all-start.4
  530.4 8.6 collective-permute-start.6
  547.7 8.7 collective-permute-start.7
  562.7 9.6 collective-permute-start.6
  615.6 8.7 collective-permute-start.6
  649.9 9.8 collective-permute-start.6
  650.0 9.8 collective-permute-start.7
  685.4 8.9 collective-permute-start.7
  700.6 9.8 collective-permute-start.6
  752.5 8.8 collective-permute-start.6
  786.7 9.7 collective-permute-start.6
  786.8 9.6 collective-permute-start.7
  800.3 10.1 all-to-all-start.5
  (114 other events, 3909.8 us)
where the time goes:
time: 1170 us
  blocking collectives  524 us (45%)
  starting transfers between devices  263 us (22%)
  waiting for transfers between devices  180 us (15%)
  loops' own time  85 us (7%)
  other arithmetic  51.5 us (4%)
  matrix products  46.7 us (4%)
    psum x1, blocking collectives, on_device(): gain_grads = lax.psum(gain_running, ('ctx', 'tp'))  354 us
    ppermute x128, starting transfers between devices, passed_along(): lax.ppermute(value, axis, [(i, (i + by) % count) for i in range(count)])  236 us
    ppermute x128, waiting for transfers between devices, passed_along(): lax.ppermute(value, axis, [(i, (i + by) % count) for i in range(count)])  159 us
    all_gather x2, blocking collectives, segment_tick(): lax.all_gather(key_local, 'ctx', axis=0, tiled=True)  87.6 us
    all_gather x2, blocking collectives, segment_tick(): lax.all_gather(value_local, 'ctx', axis=0, tiled=True)  82.4 us
    another operation x2, loops' own time, segment_tick(): lax.fori_loop(0, cycle_count, cycle_turn, (key_local, value_local, zero_k...  82.4 us
    reduce_max x33, other arithmetic, block_active(): jnp.max(key_pos) >= jnp.min(query_start)  23.7 us
  transfers between devices with their start and end apart: 135, of which 110 were waited for; matrix products, arithmetic and copies ran while one was open for 1% of the time, Pallas kernels for 0%

commit v1 on v0

v1 whole, which is shorter than its diff:
```python
import functools
import math

import jax
import jax.numpy as jnp
from jax import lax
from jax.experimental import pallas as pl
from jax.experimental.pallas import tpu as pltpu
from jax.sharding import PartitionSpec as P

HD = 128
HALF = 64
EPS = 1e-05
MASKED = -1e30
SCALE = HD ** (-0.5)
EXP2_SCALE = SCALE * math.log2(math.e)
MESH = pl.DeviceIdType.MESH
f32 = jnp.float32
bf16 = jnp.bfloat16


def remote(src, dst, send_sem, recv_sem, device):
    return pltpu.make_async_remote_copy(
        src_ref=src,
        dst_ref=dst,
        send_sem=send_sem,
        recv_sem=recv_sem,
        device_id=device,
        device_id_type=MESH,
    )


def dot_nt(a, b):
    return lax.dot_general(a, b, (((1,), (1,)), ((), ())), preferred_element_type=f32)


def dot_tn(a, b):
    return lax.dot_general(a, b, (((0,), (0,)), ((), ())), preferred_element_type=f32)


def kernel(
    dims,
    x_hbm,
    k_hbm,
    v_hbm,
    gain_ref,
    w_hbm,
    og_hbm,
    doc_ref,
    ig_out,
    dk_out,
    dv_out,
    gain_out,
    xrow,
    xh,
    ah,
    invh,
    kb,
    vb,
    qs,
    dos,
    e_ref,
    dp_ref,
    m_ref,
    l_ref,
    w_ref,
    rt_ref,
    dqt,
    dqs,
    dkf,
    dvf,
    dks,
    dvs,
    gk,
    gv,
    ig,
    cs,
    cr,
    gacc,
    gr,
    dko,
    dvo,
    local_sem,
    x_s,
    x_r,
    a_s,
    a_r,
    inv_s,
    inv_r,
    k_s,
    k_r,
    v_s,
    v_r,
    dk_s,
    dk_r,
    dv_s,
    dv_r,
    c_s,
    c_r,
    p_s,
    p_r,
    o_s,
    o_r,
    g_s,
    g_r,
    h_s,
    h_r,
):
    n_pipe, n_ctx, n_tp, ticks, group, docs = dims
    n = n_ctx
    rows = 2 * HALF // n_tp
    cols = group * HD
    width = n_tp * cols
    lanes = group * HALF
    chunk = 256
    pairs = (n + 2) // 2

    seg = lax.axis_index("pipe")
    me = lax.axis_index("ctx")
    tp = lax.axis_index("tp")
    last = n_pipe - 1
    low_pairs = (me + 2) // 2
    high_first = 2 * low_pairs

    def ctx_peer(d):
        return lax.rem(me + d, n)

    def ctx_behind(d):
        return lax.rem(me + n - d, n)

    def tp_peer(d):
        return lax.rem(tp + d, n_tp)

    def slot_of(d):
        wrapped = (n + d - 1 - me) // n
        return (1 - wrapped) * d + wrapped * (high_first + n - d)

    barrier = pltpu.get_barrier_semaphore()

    @pl.loop(1, n)
    def _(d):
        pl.semaphore_signal(barrier, inc=1, device_id={"ctx": ctx_peer(d)}, device_id_type=MESH)

    for d in range(1, n_tp):
        pl.semaphore_signal(barrier, inc=1, device_id={"tp": tp_peer(d)}, device_id_type=MESH)
    pl.semaphore_signal(
        barrier, inc=1, device_id={"pipe": lax.rem(seg + 1, n_pipe)}, device_id_type=MESH
    )
    pl.semaphore_signal(
        barrier, inc=1, device_id={"pipe": lax.rem(seg + n_pipe - 1, n_pipe)}, device_id_type=MESH
    )

    own_rows = pl.ds(pl.multiple_of(tp * rows, rows), rows)
    own_cols = pl.ds(pl.multiple_of(tp * cols, cols), cols)

    def local_copies(t):
        copies = [
            (x_hbm.at[0, t], xrow.at[t]),
            (x_hbm.at[0, t, :, own_cols], xh.at[t, own_rows, :]),
            (k_hbm.at[0, t, pl.ds(0, HALF)], kb.at[t, 0]),
            (k_hbm.at[0, t, pl.ds(HALF, HALF)], kb.at[t, high_first]),
            (v_hbm.at[0, t, pl.ds(0, HALF)], vb.at[t, 0]),
            (v_hbm.at[0, t, pl.ds(HALF, HALF)], vb.at[t, high_first]),
        ]
        if t == 0:
            copies.append((w_hbm.at[0, :, own_cols], ah.at[t, own_rows, :]))
        return [
            functools.partial(pltpu.make_async_copy, s, d, local_sem.at[t, i])
            for i, (s, d) in enumerate(copies)
        ]

    def own_output_grad(t):
        return pltpu.make_async_copy(
            og_hbm.at[t - 1, :, own_cols], ah.at[t, own_rows, :], local_sem.at[t, 6]
        )

    for t in range(ticks):
        for c in local_copies(t):
            c().start()
        if t > 0:

            @pl.when(seg == last)
            def _(t=t):
                own_output_grad(t).start()

    odd = lax.rem(me, 2)
    pad_slot = (1 - odd) * (me + 1) + odd * (n + 1)
    for t in range(ticks):
        kb[t, pad_slot] = jnp.zeros((HALF, HD), bf16)
        vb[t, pad_slot] = jnp.zeros((HALF, HD), bf16)

    for t in range(ticks):
        local_copies(t)[0]().wait()
        total = jnp.zeros((rows, HD), f32)
        for c in range(width // HD):
            x = xrow[t, :, c * HD : (c + 1) * HD].astype(f32)
            total = total + x * x
        mean = jnp.sum(total, axis=1, keepdims=True) * (1.0 / width)
        invh[t, own_rows, :] = jnp.broadcast_to(lax.rsqrt(mean + EPS), (rows, HD))

    pl.semaphore_wait(barrier, n - 1 + n_tp - 1 + 2)

    def x_send(t, d):
        to = tp_peer(d)
        there = pl.ds(pl.multiple_of(to * cols, cols), cols)
        return remote(
            x_hbm.at[0, t, :, there], xh.at[t, own_rows, :], x_s.at[t, d], x_r.at[t, d], {"tp": to}
        )

    def a_send(t, d):
        to = tp_peer(d)
        there = pl.ds(pl.multiple_of(to * cols, cols), cols)
        src = w_hbm.at[0, :, there] if t == 0 else og_hbm.at[t - 1, :, there]
        return remote(src, ah.at[t, own_rows, :], a_s.at[t, d], a_r.at[t, d], {"tp": to})

    def inv_send(t, d):
        to = tp_peer(d)
        return remote(
            invh.at[t, own_rows, :],
            invh.at[t, own_rows, :],
            inv_s.at[t, d],
            inv_r.at[t, d],
            {"tp": to},
        )

    def kv_sends(t, d):
        to = ctx_peer(d)
        wrapped = (me + d) // n
        slot = (1 - wrapped) * d + wrapped * (2 * ((to + 2) // 2) + n - d)
        section = pl.ds(pl.multiple_of(wrapped * HALF, HALF), HALF)
        return (
            remote(
                k_hbm.at[0, t, section], kb.at[t, slot], k_s.at[t, d], k_r.at[t, slot], {"ctx": to}
            ),
            remote(
                v_hbm.at[0, t, section], vb.at[t, slot], v_s.at[t, d], v_r.at[t, slot], {"ctx": to}
            ),
        )

    def send_kv(t):
        @pl.loop(1, n)
        def _(d):
            for c in kv_sends(t, d):
                c.start()

    for d in range(1, n_tp):
        inv_send(0, d).start()
        x_send(0, d).start()
        a_send(0, d).start()
    send_kv(0)
    for t in range(1, ticks):
        for d in range(1, n_tp):
            inv_send(t, d).start()
            x_send(t, d).start()

            @pl.when(seg == last)
            def _(t=t, d=d):
                a_send(t, d).start()

        send_kv(t)

    def gain_of(g):
        return gain_ref[pl.ds(tp * group + g, 1), :]

    def half_rows(h):
        return slice(h * HALF, (h + 1) * HALF)

    def head_cols(g):
        return slice(g * HD, (g + 1) * HD)

    def normed_of(t, h, g):
        return xh[t, half_rows(h), head_cols(g)].astype(f32) * invh[t, half_rows(h), :]

    def prepare(t, h):
        for g in range(group):
            at = slice(g * HALF, (g + 1) * HALF)
            qs[h, at, :] = (normed_of(t, h, g) * gain_of(g)).astype(bf16)
            dos[h, at, :] = ah[t, half_rows(h), head_cols(g)]

    def wait_slot(t, slot):
        peer = {"ctx": ctx_peer(1)}
        remote(kb.at[t, slot], kb.at[t, slot], k_s.at[t, 0], k_r.at[t, slot], peer).wait_recv()
        remote(vb.at[t, slot], vb.at[t, slot], v_s.at[t, 0], v_r.at[t, slot], peer).wait_recv()

    def wait_pair(t, p, first, count):
        for i in range(2):
            slot = 2 * p + i

            @pl.when((slot > first) & (slot < first + count))
            def _(slot=slot):
                wait_slot(t, slot)

    def pair_bounds(h):
        return (0, low_pairs) if h == 0 else (low_pairs, pairs)

    def scores(t, h):
        lane = lax.broadcasted_iota(jnp.int32, (1, lanes), 1)
        within = lax.rem(lane, HALF)
        if h == 0:
            query_pos = within + HALF * me
            start = jnp.zeros((1, lanes), jnp.int32)
            closing = jnp.int32(0)
            for k in range(docs):
                length = doc_ref[seg + t, k]
                closing = closing + length
                start = start + jnp.where(closing <= query_pos, length, 0)
            section_of_first = me
            first, count = 0, me + 1
        else:
            query_pos = within + HALF * (2 * n - 1 - me)
            start = jnp.full((1, lanes), HALF * n, jnp.int32)
            section_of_first = 2 * n - 1 - me
            first, count = high_first, n - me
        begin, end = pair_bounds(h)
        row = lax.broadcasted_iota(jnp.int32, (2 * HALF, chunk), 0)
        row = jnp.where(row < HALF, row, row - 2 * HALF)

        @pl.loop(begin, end)
        def _(p):
            wait_pair(t, p, first, count)
            key_pair = kb[t, pl.ds(2 * p, 2)].reshape(2 * HALF, HD)
            value_pair = vb[t, pl.ds(2 * p, 2)].reshape(2 * HALF, HD)
            base = HALF * (section_of_first - (2 * p - first))
            for c in range(lanes // chunk):
                at = slice(c * chunk, (c + 1) * chunk)
                s = dot_nt(key_pair, qs[h, at, :])
                upper = query_pos[:, at] - base
                lower = start[:, at] - base
                s = jnp.where((row <= upper) & (row >= lower), s, MASKED)
                peak = jnp.max(s, axis=0, keepdims=True)
                e = jnp.exp2((s - peak) * EXP2_SCALE)
                dp = dot_nt(value_pair, dos[h, at, :])
                m_ref[p, :, at] = peak
                l_ref[p, :, at] = jnp.sum(e, axis=0, keepdims=True)
                w_ref[p, :, at] = jnp.sum(e * dp, axis=0, keepdims=True)
                e_ref[p, :, at] = e
                dp_ref[p, :, at] = dp

    def combine(h):
        begin, end = pair_bounds(h)
        peak = lax.fori_loop(
            begin,
            end,
            lambda p, m: jnp.maximum(m, m_ref[p]),
            jnp.full((1, lanes), MASKED, f32),
        )

        def add(p, carry):
            total, weighted = carry
            alpha = jnp.exp2((m_ref[p] - peak) * EXP2_SCALE)
            m_ref[p] = alpha
            return total + alpha * l_ref[p], weighted + alpha * w_ref[p]

        zero = jnp.zeros((1, lanes), f32)
        total, weighted = lax.fori_loop(begin, end, add, (zero, zero))
        inverse_total = 1.0 / total
        rt_ref[h] = weighted * inverse_total

        @pl.loop(begin, end)
        def _(p):
            m_ref[p] = m_ref[p] * inverse_total

    def gradients(t, h):
        begin, end = pair_bounds(h)
        dqt[h] = jnp.zeros((HD, lanes), f32)

        @pl.loop(begin, end)
        def _(p):
            key_pair = kb[t, pl.ds(2 * p, 2)].reshape(2 * HALF, HD)
            dk = jnp.zeros((2 * HALF, HD), f32)
            dv = jnp.zeros((2 * HALF, HD), f32)
            for c in range(lanes // chunk):
                at = slice(c * chunk, (c + 1) * chunk)
                probs = e_ref[p, :, at] * m_ref[p, :, at]
                dscore = (probs * (dp_ref[p, :, at] - rt_ref[h, :, at])).astype(bf16)
                dv = dv + jnp.dot(probs.astype(bf16), dos[h, at, :], preferred_element_type=f32)
                dk = dk + jnp.dot(dscore, qs[h, at, :], preferred_element_type=f32)
                dqt[h, :, at] += dot_tn(key_pair, dscore)
            dk = (dk * SCALE).reshape(2, HALF, HD)
            dv = dv.reshape(2, HALF, HD)
            dkf[t, pl.ds(2 * p, 2)] = dk
            dvf[t, pl.ds(2 * p, 2)] = dv
            dks[t, pl.ds(2 * p, 2)] = dk.astype(bf16)
            dvs[t, pl.ds(2 * p, 2)] = dv.astype(bf16)

    def grad_sends(t, d):
        to = ctx_behind(d)
        slot = slot_of(d)
        return (
            remote(dks.at[t, slot], gk.at[t, d], dk_s.at[t, d], dk_r.at[t, d], {"ctx": to}),
            remote(dvs.at[t, slot], gv.at[t, d], dv_s.at[t, d], dv_r.at[t, d], {"ctx": to}),
        )

    def send_grads(t, h):
        begin, end = (1, me + 1) if h == 0 else (me + 1, n)

        @pl.loop(begin, end)
        def _(d):
            for c in grad_sends(t, d):
                c.start()

    def coupling_send(t, h, d):
        return remote(
            cs.at[t, h], cr.at[t, h, d], c_s.at[t, h, d], c_r.at[t, h, d], {"tp": tp_peer(d)}
        )

    def couple(t, h):
        dq = jnp.transpose(dqt[h] * SCALE)
        low = dq.astype(bf16)
        dqs[h] = low
        part = jnp.zeros((HALF, HD), f32)
        for g in range(group):
            rounded = low[g * HALF : (g + 1) * HALF, :].astype(f32)
            product = rounded * normed_of(t, h, g)
            gacc[pl.ds(g, 1), :] += jnp.sum(product, axis=0, keepdims=True)
            part = part + product * gain_of(g)
        part = jnp.sum(part, axis=1, keepdims=True)
        cs[t, h] = jnp.broadcast_to(part, (HALF, HD))
        for d in range(1, n_tp):
            coupling_send(t, h, d).start()

    def pipe_send(t, h):
        there = ah.at[t + 1, half_rows(h), :]
        return remote(
            ig.at[t, half_rows(h), :],
            there,
            p_s.at[t, h],
            p_r.at[t, h],
            {"pipe": lax.rem(seg + n_pipe - 1, n_pipe)},
        )

    def out_send(t, j):
        d = lax.rem(j + n_tp - tp, n_tp)
        return remote(
            ig.at[t, j * rows : (j + 1) * rows, :],
            ig_out.at[0, t, :, own_cols],
            o_s.at[t, d],
            o_r.at[t, d],
            {"tp": j},
        )

    def out_own(t):
        return pltpu.make_async_copy(
            ig.at[t, own_rows, :], ig_out.at[0, t, :, own_cols], o_s.at[t, 0]
        )

    per_half = n_tp // 2

    def finish(t, h):
        total = cs[t, h]
        for d in range(1, n_tp):
            coupling_send(t, h, d).wait_recv()
            total = total + cr[t, h, d]
        coupling = total * (1.0 / width)
        for g in range(group):
            normed = normed_of(t, h, g)
            scaled = dqs[h, g * HALF : (g + 1) * HALF, :].astype(f32) * gain_of(g)
            arriving = ah[t, half_rows(h), head_cols(g)].astype(f32)
            result = arriving + invh[t, half_rows(h), :] * (scaled - normed * coupling)
            ig[t, half_rows(h), head_cols(g)] = result.astype(bf16)
        if t + 1 < ticks:

            @pl.when(seg > 0)
            def _():
                pipe_send(t, h).start()

        for j in range(h * per_half, (h + 1) * per_half):

            @pl.when(tp != j)
            def _(j=j):
                out_send(t, j).start()

            @pl.when(tp == j)
            def _():
                out_own(t).start()

    gacc[...] = jnp.zeros((group, HD), f32)
    for t in range(ticks):
        for c in local_copies(t)[1:]:
            c().wait()
        for d in range(1, n_tp):
            inv_send(t, d).wait_recv()
            x_send(t, d).wait_recv()
        if t == 0:
            for d in range(1, n_tp):
                a_send(t, d).wait_recv()
        else:

            @pl.when(seg == last)
            def _(t=t):
                own_output_grad(t).wait()
                for d in range(1, n_tp):
                    a_send(t, d).wait_recv()

        for h in range(2):
            if t > 0:

                @pl.when(seg < last)
                def _(t=t, h=h):
                    pipe_send(t - 1, h).wait_recv()

            prepare(t, h)
            scores(t, h)
        for h in range(2):
            combine(h)
            gradients(t, h)
            send_grads(t, h)
            couple(t, h)
        for h in range(2):
            finish(t, h)

    def gain_send(d):
        return remote(gacc, gr.at[d], g_s.at[d], g_r.at[d], {"ctx": ctx_peer(d)})

    @pl.loop(1, n)
    def _(d):
        gain_send(d).start()

    def result_copies(t):
        return (
            pltpu.make_async_copy(dko.at[t], dk_out.at[0, t], local_sem.at[t, 7]),
            pltpu.make_async_copy(dvo.at[t], dv_out.at[0, t], local_sem.at[t, 8]),
        )

    for t in range(ticks):
        for i, (mine, at) in enumerate(((0, slice(0, HALF)), (high_first, slice(HALF, 2 * HALF)))):
            begin, end = (1, n - me) if i == 0 else (n - me, n)

            def add(d, carry, t=t):
                for c in grad_sends(t, d):
                    c.wait_recv()
                return (carry[0] + gk[t, d].astype(f32), carry[1] + gv[t, d].astype(f32))

            dk, dv = lax.fori_loop(begin, end, add, (dkf[t, mine], dvf[t, mine]))
            dko[t, at, :] = dk
            dvo[t, at, :] = dv
        for c in result_copies(t):
            c.start()

    def add_gain(d, total):
        gain_send(d).wait_recv()
        return total + gr[d]

    gain_total = lax.fori_loop(1, n, add_gain, gacc[...])
    gr[0] = gain_total
    own_gain = pl.ds(pl.multiple_of(tp * group, group), group)

    def gain_share(d):
        return remote(
            gr.at[0], gain_out.at[own_gain, :], h_s.at[d], h_r.at[d], {"tp": tp_peer(d)}
        )

    own_gain_copy = pltpu.make_async_copy(gr.at[0], gain_out.at[own_gain, :], h_s.at[0])
    own_gain_copy.start()
    for d in range(1, n_tp):
        gain_share(d).start()

    for t in range(ticks):
        for d in range(1, n_tp):
            inv_send(t, d).wait_send()
            x_send(t, d).wait_send()
            if t == 0:
                a_send(t, d).wait_send()
            else:

                @pl.when(seg == last)
                def _(t=t, d=d):
                    a_send(t, d).wait_send()

            for h in range(2):
                coupling_send(t, h, d).wait_send()

        @pl.loop(1, n)
        def _(d, t=t):
            for c in kv_sends(t, d):
                c.wait_send()
            for c in grad_sends(t, d):
                c.wait_send()

        if t + 1 < ticks:
            for h in range(2):

                @pl.when(seg > 0)
                def _(t=t, h=h):
                    pipe_send(t, h).wait_send()

        for j in range(n_tp):

            @pl.when(tp != j)
            def _(t=t, j=j):
                out_send(t, j).wait_send()

            @pl.when(tp == j)
            def _(t=t):
                out_own(t).wait()

        for d in range(1, n_tp):
            came = ig_out.at[0, t, :, own_cols]
            remote(came, came, o_s.at[t, d], o_r.at[t, d], {"tp": tp_peer(d)}).wait_recv()
        for c in result_copies(t):
            c.wait()

    @pl.loop(1, n)
    def _(d):
        gain_send(d).wait_send()

    own_gain_copy.wait()
    for d in range(1, n_tp):
        gain_share(d).wait_send()
        gain_share(d).wait_recv()


def solution(mesh):
    n_pipe, n_ctx, n_tp = (mesh.shape[a] for a in ("pipe", "ctx", "tp"))

    def on_device(segment_inputs, keys, values, norm_gain, waiting_grads, output_grads, doc_lengths):
        ticks, rows, width = segment_inputs.shape[1:]
        cols = width // n_tp
        group = cols // HD
        docs = doc_lengths.shape[1]
        lanes = group * HALF
        slots = n_ctx + 2
        pairs = slots // 2
        dims = (n_pipe, n_ctx, n_tp, ticks, group, docs)
        dma = pltpu.SemaphoreType.DMA
        vmem = pltpu.VMEM
        hbm = pl.BlockSpec(memory_space=pl.ANY)
        scratch = [
            vmem((ticks, rows, width), bf16),
            vmem((ticks, 2 * HALF, cols), bf16),
            vmem((ticks, 2 * HALF, cols), bf16),
            vmem((ticks, 2 * HALF, HD), f32),
            vmem((ticks, slots, HALF, HD), bf16),
            vmem((ticks, slots, HALF, HD), bf16),
            vmem((2, lanes, HD), bf16),
            vmem((2, lanes, HD), bf16),
            vmem((pairs, 2 * HALF, lanes), f32),
            vmem((pairs, 2 * HALF, lanes), f32),
            vmem((pairs, 1, lanes), f32),
            vmem((pairs, 1, lanes), f32),
            vmem((pairs, 1, lanes), f32),
            vmem((2, 1, lanes), f32),
            vmem((2, HD, lanes), f32),
            vmem((2, lanes, HD), bf16),
            vmem((ticks, slots, HALF, HD), f32),
            vmem((ticks, slots, HALF, HD), f32),
            vmem((ticks, slots, HALF, HD), bf16),
            vmem((ticks, slots, HALF, HD), bf16),
            vmem((ticks, n_ctx, HALF, HD), bf16),
            vmem((ticks, n_ctx, HALF, HD), bf16),
            vmem((ticks, 2 * HALF, cols), bf16),
            vmem((ticks, 2, HALF, HD), f32),
            vmem((ticks, 2, n_tp, HALF, HD), f32),
            vmem((group, HD), f32),
            vmem((n_ctx, group, HD), f32),
            vmem((ticks, 2 * HALF, HD), f32),
            vmem((ticks, 2 * HALF, HD), f32),
            dma((ticks, 9)),
            dma((ticks, n_tp)),
            dma((ticks, n_tp)),
            dma((ticks, n_tp)),
            dma((ticks, n_tp)),
            dma((ticks, n_tp)),
            dma((ticks, n_tp)),
            dma((ticks, n_ctx)),
            dma((ticks, slots)),
            dma((ticks, n_ctx)),
            dma((ticks, slots)),
            dma((ticks, n_ctx)),
            dma((ticks, n_ctx)),
            dma((ticks, n_ctx)),
            dma((ticks, n_ctx)),
            dma((ticks, 2, n_tp)),
            dma((ticks, 2, n_tp)),
            dma((ticks, 2)),
            dma((ticks, 2)),
            dma((ticks, n_tp)),
            dma((ticks, n_tp)),
            dma((n_ctx,)),
            dma((n_ctx,)),
            dma((n_tp,)),
            dma((n_tp,)),
        ]
        input_grads, key_grads, value_grads, gain_grads = pl.pallas_call(
            functools.partial(kernel, dims),
            out_shape=(
                jax.ShapeDtypeStruct((1, ticks, rows, width), bf16),
                jax.ShapeDtypeStruct((1, ticks, 2 * HALF, HD), f32),
                jax.ShapeDtypeStruct((1, ticks, 2 * HALF, HD), f32),
                jax.ShapeDtypeStruct((width // HD, HD), f32),
            ),
            in_specs=[
                hbm,
                hbm,
                hbm,
                pl.BlockSpec(memory_space=pltpu.VMEM),
                hbm,
                hbm,
                pl.BlockSpec(memory_space=pltpu.SMEM),
            ],
            out_specs=(hbm, hbm, hbm, hbm),
            scratch_shapes=scratch,
            compiler_params=pltpu.CompilerParams(
                collective_id=0, has_side_effects=True, vmem_limit_bytes=48 << 20
            ),
            name="window",
        )(
            segment_inputs,
            keys,
            values,
            norm_gain.reshape(width // HD, HD),
            waiting_grads,
            output_grads,
            doc_lengths,
        )
        return input_grads, key_grads, value_grads, gain_grads.reshape(1, width)

    in_specs = (
        P("pipe", None, ("ctx", "tp"), None),
        P("pipe", None, "ctx", "tp"),
        P("pipe", None, "ctx", "tp"),
        P("pipe", None),
        P("pipe", ("ctx", "tp"), None),
        P(None, ("ctx", "tp"), None),
        P(),
    )
    out_specs = (
        P("pipe", None, ("ctx", "tp"), None),
        P("pipe", None, "ctx", "tp"),
        P("pipe", None, "ctx", "tp"),
        P("pipe", None),
    )
    return jax.shard_map(
        on_device, mesh=mesh, in_specs=in_specs, out_specs=out_specs, check_vma=False
    )
```

time: 1170 us -> 79.7 us (0.07)
  the two profiles are of different devices: /device:TPU:8 before, /device:TPU:1 now
where the time goes in v1:
time: 79.7 us; the launch traced here: 79.3 us
  Pallas kernels  70 us (88%)
  local copies, waits for them, and re-layouts  8.72 us (11%)
    pallas_call x1, Pallas kernels, on_device(): pl.pallas_call(functools.partial(kernel, dims), out_shape=(jax.ShapeDtype...  70 us
    unnamed x18, local copies, waits for them, and re-layouts  8.72 us

profile of v1, /device:TPU:1, one launch (start us, length us, event | category | flops | bytes accessed | tf_op | source)
XLA Modules:
  0.0 79.3 jit_solution(13535995552813553961)
XLA Ops:
  0.6 0.0 copy-start
  0.6 1.0 %copy-done = bf16[1,2,32,4096]{3,2,1,0:T(8,128)(2,1)S(1)} copy-done((bf16[1,2,32,4096]{3,2,1,0:T(8,128)(2,1)S(1)}, bf16[1,2,32,4096]{3,2,1,0:T(8,128)(2,1)}, u32[]{:S(2)}) %copy-start) | copy-done | bytes 524312
  1.7 0.0 copy-start.1
  1.7 0.9 %copy-done.1 = bf16[1,32,4096]{2,1,0:T(8,128)(2,1)S(1)} copy-done((bf16[1,32,4096]{2,1,0:T(8,128)(2,1)S(1)}, bf16[1,32,4096]{2,1,0:T(8,128)(2,1)}, u32[]{:S(2)}) %copy-start.1) | copy-done | bytes 262168
  2.6 0.0 copy-start.2
  2.6 0.9 %copy-done.2 = bf16[1,32,4096]{2,1,0:T(8,128)(2,1)S(1)} copy-done((bf16[1,32,4096]{2,1,0:T(8,128)(2,1)S(1)}, bf16[1,32,4096]{2,1,0:T(8,128)(2,1)}, u32[]{:S(2)}) %copy-start.2) | copy-done | bytes 262168
  3.6 0.0 copy-start.3
  3.6 0.8 %copy-done.3 = bf16[1,2,128,128]{3,2,1,0:T(8,128)(2,1)S(1)} copy-done((bf16[1,2,128,128]{3,2,1,0:T(8,128)(2,1)S(1)}, bf16[1,2,128,128]{3,2,1,0:T(8,128)(2,1)}, u32[]{:S(2)}) %copy-start.3) | copy-done | bytes 65560
  4.4 0.0 copy-start.4
  4.4 0.8 %copy-done.4 = bf16[1,2,128,128]{3,2,1,0:T(8,128)(2,1)S(1)} copy-done((bf16[1,2,128,128]{3,2,1,0:T(8,128)(2,1)S(1)}, bf16[1,2,128,128]{3,2,1,0:T(8,128)(2,1)}, u32[]{:S(2)}) %copy-start.4) | copy-done | bytes 65560
  5.3 0.0 copy-start.5
  5.3 0.7 copy-done.5
  6.0 0.0 copy-start.6
  6.0 0.7 copy-done.6
  6.7 70.0 %window.1 = (bf16[1,2,32,4096]{3,2,1,0:T(8,128)(2,1)S(1)}, f32[1,2,128,128]{3,2,1,0:T(8,128)S(1)}, f32[1,2,128,128]{3,2,1,0:T(8,128)S(1)}, f32[32,128]{1,0:T(8,128)S(1)}) custom-call(bf16[1,2,32,4096]{3,2,1,0:T(8,128)(2,1)S(1)} %copy-done, bf16[1,2,128,128]{3,2,1,0:T(8,128)(2,1)S(1)} %copy-done.3, bf16[1,2,128,128]{3,2,1,0:T(8,128)(2,1)S(1)} %copy-done.4, ...), custom_call_target="tpu_custom_call" | custom-call | tf_op jit(solution)/shard_map/window/pallas_call | solution.py:684
  76.6 0.8 %copy.15 = bf16[1,2,32,4096]{3,2,1,0:T(8,128)(2,1)} copy(bf16[1,2,32,4096]{3,2,1,0:T(8,128)(2,1)S(1)} %get-tuple-element.16) | data formatting | bytes 1048576
  77.4 0.7 copy.16
  78.1 0.7 copy.17
  78.7 0.6 copy.18
Async XLA Ops:
  0.6 1.0 %copy-start = (bf16[1,2,32,4096]{3,2,1,0:T(8,128)(2,1)S(1)}, bf16[1,2,32,4096]{3,2,1,0:T(8,128)(2,1)}, u32[]{:S(2)}) copy-start(bf16[1,2,32,4096]{3,2,1,0:T(8,128)(2,1)} %x_hbm.1) | copy-start | bytes 1572868
  1.7 0.9 %copy-start.1 = (bf16[1,32,4096]{2,1,0:T(8,128)(2,1)S(1)}, bf16[1,32,4096]{2,1,0:T(8,128)(2,1)}, u32[]{:S(2)}) copy-start(bf16[1,32,4096]{2,1,0:T(8,128)(2,1)} %w_hbm.1) | copy-start | bytes 786436
  2.6 0.9 %copy-start.2 = (bf16[1,32,4096]{2,1,0:T(8,128)(2,1)S(1)}, bf16[1,32,4096]{2,1,0:T(8,128)(2,1)}, u32[]{:S(2)}) copy-start(bf16[1,32,4096]{2,1,0:T(8,128)(2,1)} %og_hbm.1) | copy-start | bytes 786436
  3.6 0.8 %copy-start.3 = (bf16[1,2,128,128]{3,2,1,0:T(8,128)(2,1)S(1)}, bf16[1,2,128,128]{3,2,1,0:T(8,128)(2,1)}, u32[]{:S(2)}) copy-start(bf16[1,2,128,128]{3,2,1,0:T(8,128)(2,1)} %k_hbm.1) | copy-start | bytes 196612
  4.4 0.8 %copy-start.4 = (bf16[1,2,128,128]{3,2,1,0:T(8,128)(2,1)S(1)}, bf16[1,2,128,128]{3,2,1,0:T(8,128)(2,1)}, u32[]{:S(2)}) copy-start(bf16[1,2,128,128]{3,2,1,0:T(8,128)(2,1)} %v_hbm.1) | copy-start | bytes 196612
  5.3 0.7 copy-start.5
  6.0 0.7 copy-start.6

commit v2 on v1

v2 whole, which is shorter than its diff:
```python
import functools
import math

import jax
import jax.numpy as jnp
from jax import lax
from jax.experimental import pallas as pl
from jax.experimental.pallas import tpu as pltpu
from jax.sharding import PartitionSpec as P

HD = 128
HALF = 64
EPS = 1e-05
MASKED = -1e30
SCALE = HD ** (-0.5)
EXP2_SCALE = SCALE * math.log2(math.e)
KERNEL_VMEM = 60 << 20
MESH = pl.DeviceIdType.MESH
f32 = jnp.float32
bf16 = jnp.bfloat16


def remote(src, dst, send_sem, recv_sem, device):
    return pltpu.make_async_remote_copy(
        src_ref=src,
        dst_ref=dst,
        send_sem=send_sem,
        recv_sem=recv_sem,
        device_id=device,
        device_id_type=MESH,
    )


def dot_nt(a, b):
    return lax.dot_general(a, b, (((1,), (1,)), ((), ())), preferred_element_type=f32)


def dot_tn(a, b):
    return lax.dot_general(a, b, (((0,), (0,)), ((), ())), preferred_element_type=f32)


def kernel(
    dims,
    x_hbm,
    k_hbm,
    v_hbm,
    gain_ref,
    w_hbm,
    og_hbm,
    doc_ref,
    ig_out,
    dk_out,
    dv_out,
    gain_out,
    xrow,
    xh,
    ah,
    invh,
    kv,
    qs,
    dos,
    e_ref,
    dp_ref,
    m_ref,
    l_ref,
    rt_ref,
    dqt,
    dqs,
    gf,
    gb,
    gp,
    gs,
    gz,
    ig,
    cs,
    cr,
    gacc,
    gr,
    res,
    local_sem,
    x_s,
    x_r,
    a_s,
    a_r,
    inv_s,
    inv_r,
    kv_s,
    kv_r,
    fw_s,
    gp_s,
    gp_r,
    gz_s,
    gz_r,
    c_s,
    c_r,
    p_s,
    p_r,
    o_s,
    o_r,
    g_s,
    g_r,
    h_s,
    h_r,
):
    n_pipe, n_ctx, n_tp, ticks, group, docs = dims
    n = n_ctx
    rows = 2 * HALF // n_tp
    cols = group * HD
    width = n_tp * cols
    lanes = group * HALF
    chunk = 256
    pairs = (n + 2) // 2

    seg = lax.axis_index("pipe")
    me = lax.axis_index("ctx")
    tp = lax.axis_index("tp")
    last = n_pipe - 1
    low_pairs = (me + 2) // 2
    high_first = 2 * low_pairs

    def ctx_peer(d):
        return lax.rem(me + d, n)

    def ctx_behind(d):
        return lax.rem(me + n - d, n)

    def tp_peer(d):
        return lax.rem(tp + d, n_tp)

    line = lax.rem(me, 2)
    partner = me + 1 - 2 * line
    lines = n // 2
    far_first = sorted(range(1, lines), key=lambda i: -min(i, lines - i))

    def upper(d):
        return (n + d - 1 - me) // n

    def slot_of(d):
        return (1 - upper(d)) * d + upper(d) * (high_first + n - d)

    def partner_slot(slot, is_upper):
        return slot + (1 - 2 * line) * (1 - 2 * is_upper)

    barrier = pltpu.get_barrier_semaphore()

    @pl.loop(1, n)
    def _(d):
        pl.semaphore_signal(barrier, inc=1, device_id={"ctx": ctx_peer(d)}, device_id_type=MESH)

    for d in range(1, n_tp):
        pl.semaphore_signal(barrier, inc=1, device_id={"tp": tp_peer(d)}, device_id_type=MESH)
    pl.semaphore_signal(
        barrier, inc=1, device_id={"pipe": lax.rem(seg + 1, n_pipe)}, device_id_type=MESH
    )
    pl.semaphore_signal(
        barrier, inc=1, device_id={"pipe": lax.rem(seg + n_pipe - 1, n_pipe)}, device_id_type=MESH
    )

    own_rows = pl.ds(pl.multiple_of(tp * rows, rows), rows)
    own_cols = pl.ds(pl.multiple_of(tp * cols, cols), cols)

    def kv_copies(t):
        return [
            pltpu.make_async_copy(
                ref.at[0, t, pl.ds(i * HALF, HALF)], kv.at[t, slot, which], local_sem.at[t, 2 * which + i]
            )
            for which, ref in enumerate((k_hbm, v_hbm))
            for i, slot in enumerate((0, high_first))
        ]

    def x_copy(t):
        return pltpu.make_async_copy(x_hbm.at[0, t], xrow.at[t], local_sem.at[t, 4])

    def own_x(t):
        return pltpu.make_async_copy(
            x_hbm.at[0, t, :, own_cols], xh.at[t, own_rows, :], local_sem.at[t, 5]
        )

    def own_a(t):
        return pltpu.make_async_copy(
            w_hbm.at[0, :, own_cols], ah.at[t, own_rows, :], local_sem.at[t, 6]
        )

    def own_output_grad(t):
        return pltpu.make_async_copy(
            og_hbm.at[t - 1, :, own_cols], ah.at[t, own_rows, :], local_sem.at[t, 6]
        )

    for t in range(ticks):
        for c in kv_copies(t):
            c.start()
    for t in range(ticks):
        x_copy(t).start()
        own_x(t).start()
        if t == 0:
            own_a(t).start()
        else:

            @pl.when(seg == last)
            def _(t=t):
                own_output_grad(t).start()

    odd = lax.rem(me, 2)
    pad_slot = (1 - odd) * (me + 1) + odd * (n + 1)
    for t in range(ticks):
        kv[t, pad_slot] = jnp.zeros((2, HALF, HD), bf16)
    for t in range(ticks):
        for c in kv_copies(t):
            c.wait()

    pl.semaphore_wait(barrier, n - 1 + n_tp - 1 + 2)

    def x_send(t, d):
        to = tp_peer(d)
        there = pl.ds(pl.multiple_of(to * cols, cols), cols)
        return remote(
            x_hbm.at[0, t, :, there], xh.at[t, own_rows, :], x_s.at[t, d], x_r.at[t, d], {"tp": to}
        )

    def a_send(t, d):
        to = tp_peer(d)
        there = pl.ds(pl.multiple_of(to * cols, cols), cols)
        src = w_hbm.at[0, :, there] if t == 0 else og_hbm.at[t - 1, :, there]
        return remote(src, ah.at[t, own_rows, :], a_s.at[t, d], a_r.at[t, d], {"tp": to})

    def inv_send(t, d):
        to = tp_peer(d)
        return remote(
            invh.at[t, own_rows, :],
            invh.at[t, own_rows, :],
            inv_s.at[t, d],
            inv_r.at[t, d],
            {"tp": to},
        )

    def kv_send(t, which, i):
        d = 2 * i
        to = ctx_peer(d)
        wrapped = (me + d) // n
        slot = (1 - wrapped) * d + wrapped * (2 * ((to + 2) // 2) + n - d)
        return remote(
            kv.at[t, wrapped * high_first, which],
            kv.at[t, slot, which],
            kv_s.at[t, which, i],
            kv_r.at[t, which, slot],
            {"ctx": to},
        )

    def kv_forward(t, which, i):
        if i == 0:
            slot, is_upper = line * high_first, line
        else:
            slot, is_upper = slot_of(2 * i), upper(2 * i)
        there = partner_slot(slot, is_upper)
        return remote(
            kv.at[t, slot, which],
            kv.at[t, there, which],
            fw_s.at[t, which, i],
            kv_r.at[t, which, there],
            {"ctx": partner},
        )

    def kv_wait(t, which, slot):
        came = kv.at[t, slot, which]
        remote(
            came, came, kv_s.at[t, which, 0], kv_r.at[t, which, slot], {"ctx": partner}
        ).wait_recv()

    def send_kv(t, which):
        kv_forward(t, which, 0).start()
        for i in far_first:
            kv_send(t, which, i).start()

    def forward_kv(t, which):
        for i in far_first:
            kv_wait(t, which, slot_of(2 * i))
            kv_forward(t, which, i).start()

    def inverse(t):
        x_copy(t).wait()
        total = jnp.zeros((rows, HD), f32)
        for c in range(width // HD):
            x = xrow[t, :, c * HD : (c + 1) * HD].astype(f32)
            total = total + x * x
        mean = jnp.sum(total, axis=1, keepdims=True) * (1.0 / width)
        invh[t, own_rows, :] = jnp.broadcast_to(lax.rsqrt(mean + EPS), (rows, HD))
        for d in range(1, n_tp):
            inv_send(t, d).start()

    for t in range(ticks):
        for which in range(2):
            send_kv(t, which)
        inverse(t)
        for d in range(1, n_tp):
            x_send(t, d).start()
        for d in range(1, n_tp):
            if t == 0:
                a_send(t, d).start()
            else:

                @pl.when(seg == last)
                def _(t=t, d=d):
                    a_send(t, d).start()

    def gain_of(g):
        return gain_ref[pl.ds(tp * group + g, 1), :]

    def half_rows(h):
        return slice(h * HALF, (h + 1) * HALF)

    def head_cols(g):
        return slice(g * HD, (g + 1) * HD)

    def normed_of(t, h, g):
        return xh[t, half_rows(h), head_cols(g)].astype(f32) * invh[t, half_rows(h), :]

    def head_rows(g):
        return slice(g * HALF, (g + 1) * HALF)

    def prepare_queries(t, h):
        for g in range(group):
            qs[t, h, head_rows(g), :] = (normed_of(t, h, g) * gain_of(g)).astype(bf16)

    def prepare_arriving(t, h):
        for g in range(group):
            dos[h, head_rows(g), :] = ah[t, half_rows(h), head_cols(g)]

    unroll = 3 if pairs % 3 == 0 else 1

    def each_group(step):
        @pl.loop(0, pairs // unroll)
        def _(i):
            step([i * unroll + u for u in range(unroll)])

    def half_of(p):
        return (p - low_pairs + n) // n

    def pair_of(t, p, which):
        return kv[t, pl.ds(2 * p, 2), which].reshape(2 * HALF, HD)

    chunks = [slice(c * chunk, (c + 1) * chunk) for c in range(lanes // chunk)]

    def wait_forwarded(t, which, p):
        h = half_of(p)

        @pl.when(2 * p + 1 < (1 - h) * (me + 1) + h * (high_first + n - me))
        def _():
            kv_wait(t, which, 2 * p + 1)

    def by_half(values, combine, empty):
        result = [jnp.full((1, lanes), empty, f32) for _ in range(2)]
        for p, value in enumerate(values):
            is_low = p < low_pairs
            result[0] = combine(result[0], jnp.where(is_low, value, empty))
            result[1] = combine(result[1], jnp.where(is_low, empty, value))
        return result

    def softmax(t):
        within = lax.rem(lax.broadcasted_iota(jnp.int32, (1, lanes), 1), HALF)
        low_pos = within + HALF * me
        low_start = jnp.zeros((1, lanes), jnp.int32)
        closing = jnp.int32(0)
        for k in range(docs):
            length = doc_ref[seg + t, k]
            closing = closing + length
            low_start = low_start + jnp.where(closing <= low_pos, length, 0)
        row = lax.broadcasted_iota(jnp.int32, (2 * HALF, chunk), 0)
        row = jnp.where(row < HALF, row, row - 2 * HALF)

        def step(group_pairs):
            for p in group_pairs:
                wait_forwarded(t, 0, p)
            for p in group_pairs:
                h = half_of(p)
                section = (1 - h) * me + h * (2 * n - 1 - me)
                base = HALF * (section - (2 * p - h * high_first))
                up_to = within + (HALF * section - base)
                down_to = jnp.where(h == 0, low_start, HALF * n) - base
                key_pair = pair_of(t, p, 0)
                for at in chunks:
                    s = dot_nt(key_pair, qs[t, h, at, :])
                    s = jnp.where((row <= up_to[:, at]) & (row >= down_to[:, at]), s, MASKED)
                    peak = jnp.max(s, axis=0, keepdims=True)
                    e = jnp.exp2((s - peak) * EXP2_SCALE)
                    m_ref[t, p, :, at] = peak
                    l_ref[p, :, at] = jnp.sum(e, axis=0, keepdims=True)
                    e_ref[t, p, :, at] = e

        each_group(step)
        peaks = [m_ref[t, p] for p in range(pairs)]
        peak = by_half(peaks, jnp.maximum, MASKED)
        alphas = [
            jnp.exp2((m - jnp.where(p < low_pairs, peak[0], peak[1])) * EXP2_SCALE)
            for p, m in enumerate(peaks)
        ]
        total = by_half([a * l_ref[p] for p, a in enumerate(alphas)], jnp.add, 0.0)
        inverse_total = [1.0 / part for part in total]
        for p, alpha in enumerate(alphas):
            m_ref[t, p] = alpha * jnp.where(p < low_pairs, inverse_total[0], inverse_total[1])

    def put_gradient(t, p, which, value):
        value = value.reshape(2, HALF, HD)
        gf[t, pl.ds(2 * p, 2), which] = value
        gb[t, pl.ds(2 * p, 2), which] = value.astype(bf16)

    def values_pass(t):
        def step(group_pairs):
            for p in group_pairs:
                wait_forwarded(t, 1, p)
            for p in group_pairs:
                h = half_of(p)
                value_pair = pair_of(t, p, 1)
                dv = jnp.zeros((2 * HALF, HD), f32)
                for at in chunks:
                    grads = dos[h, at, :]
                    probs = e_ref[t, p, :, at] * m_ref[t, p, :, at]
                    dp = dot_nt(value_pair, grads)
                    dv = dv + jnp.dot(probs.astype(bf16), grads, preferred_element_type=f32)
                    l_ref[p, :, at] = jnp.sum(probs * dp, axis=0, keepdims=True)
                    dp_ref[p, :, at] = dp
                put_gradient(t, p, 1, dv)

        each_group(step)
        terms = by_half([l_ref[p] for p in range(pairs)], jnp.add, 0.0)
        for h in range(2):
            rt_ref[h] = terms[h]

    def keys_pass(t):
        for h in range(2):
            dqt[h] = jnp.zeros((HD, lanes), f32)

        def step(group_pairs):
            for p in group_pairs:
                h = half_of(p)
                key_pair = pair_of(t, p, 0)
                dk = jnp.zeros((2 * HALF, HD), f32)
                for at in chunks:
                    probs = e_ref[t, p, :, at] * m_ref[t, p, :, at]
                    dscore = (probs * (dp_ref[p, :, at] - rt_ref[h, :, at])).astype(bf16)
                    dk = dk + jnp.dot(dscore, qs[t, h, at, :], preferred_element_type=f32)
                    dqt[h, :, at] += dot_tn(key_pair, dscore)
                put_gradient(t, p, 0, dk * SCALE)

        each_group(step)

    def partner_send(t, which, i):
        d = 2 * i + 1
        slot = slot_of(d)
        there = partner_slot(slot, upper(d))
        return remote(
            gb.at[t, slot, which],
            gp.at[t, there, which],
            gp_s.at[t, which, i],
            gp_r.at[t, which, there],
            {"ctx": partner},
        )

    def send_to_partner(t, which):
        @pl.loop(0, lines)
        def _(i):
            partner_send(t, which, i).start()

    def partner_wait(t, which, slot):
        came = gp.at[t, slot, which]
        remote(
            came, came, gp_s.at[t, which, 0], gp_r.at[t, which, slot], {"ctx": partner}
        ).wait_recv()

    def owner_send(t, which, i):
        return remote(
            gs.at[t, i, which],
            gz.at[t, i, which],
            gz_s.at[t, which, i],
            gz_r.at[t, which, i],
            {"ctx": ctx_behind(2 * i)},
        )

    def send_to_owners(t, which):
        for i in far_first:
            slot = slot_of(2 * i)
            partner_wait(t, which, slot)
            both = gf[t, slot, which] + gp[t, slot, which].astype(f32)
            gs[t, i, which] = both.astype(bf16)
            owner_send(t, which, i).start()

    def coupling_send(t, h, d):
        return remote(
            cs.at[t, h], cr.at[t, h, d], c_s.at[t, h, d], c_r.at[t, h, d], {"tp": tp_peer(d)}
        )

    diagonal = lax.broadcasted_iota(jnp.int32, (HALF, HD), 0) == lax.broadcasted_iota(
        jnp.int32, (HALF, HD), 1
    )

    def couple(t, h):
        dq = jnp.transpose(dqt[h] * SCALE)
        low = dq.astype(bf16)
        dqs[h] = low
        part = jnp.zeros((HALF, HD), f32)
        for g in range(group):
            rounded = low[g * HALF : (g + 1) * HALF, :].astype(f32)
            product = rounded * normed_of(t, h, g)
            gacc[pl.ds(g, 1), :] += jnp.sum(product, axis=0, keepdims=True)
            part = part + product * gain_of(g)
        part = jnp.sum(part, axis=1, keepdims=True)
        cs[t, h] = jnp.sum(jnp.where(diagonal, part, 0.0), axis=0, keepdims=True)
        for d in range(1, n_tp):
            coupling_send(t, h, d).start()

    def pipe_send(t, h):
        there = ah.at[t + 1, half_rows(h), :]
        return remote(
            ig.at[t, half_rows(h), :],
            there,
            p_s.at[t, h],
            p_r.at[t, h],
            {"pipe": lax.rem(seg + n_pipe - 1, n_pipe)},
        )

    def out_send(t, j):
        d = lax.rem(j + n_tp - tp, n_tp)
        return remote(
            ig.at[t, j * rows : (j + 1) * rows, :],
            ig_out.at[0, t, :, own_cols],
            o_s.at[t, d],
            o_r.at[t, d],
            {"tp": j},
        )

    def out_own(t):
        return pltpu.make_async_copy(
            ig.at[t, own_rows, :], ig_out.at[0, t, :, own_cols], o_s.at[t, 0]
        )

    per_half = n_tp // 2

    def finish(t, h):
        total = cs[t, h]
        for d in range(1, n_tp):
            coupling_send(t, h, d).wait_recv()
            total = total + cr[t, h, d]
        coupling = jnp.sum(jnp.where(diagonal, total, 0.0), axis=1, keepdims=True) * (1.0 / width)
        for g in range(group):
            normed = normed_of(t, h, g)
            scaled = dqs[h, g * HALF : (g + 1) * HALF, :].astype(f32) * gain_of(g)
            arriving = ah[t, half_rows(h), head_cols(g)].astype(f32)
            result = arriving + invh[t, half_rows(h), :] * (scaled - normed * coupling)
            ig[t, half_rows(h), head_cols(g)] = result.astype(bf16)
        if t + 1 < ticks:

            @pl.when(seg > 0)
            def _():
                pipe_send(t, h).start()

        for j in range(h * per_half, (h + 1) * per_half):

            @pl.when(tp != j)
            def _(j=j):
                out_send(t, j).start()

            @pl.when(tp == j)
            def _():
                out_own(t).start()

    gacc[...] = jnp.zeros((group, HD), f32)

    def wait_rows(t):
        own_x(t).wait()
        for d in range(1, n_tp):
            inv_send(t, d).wait_recv()
            x_send(t, d).wait_recv()

    def wait_arriving(t, h):
        if t == 0:
            if h == 0:
                own_a(t).wait()
                for d in range(1, n_tp):
                    a_send(t, d).wait_recv()
            return

        @pl.when(seg < last)
        def _():
            pipe_send(t - 1, h).wait_recv()

        if h == 0:

            @pl.when(seg == last)
            def _():
                own_output_grad(t).wait()
                for d in range(1, n_tp):
                    a_send(t, d).wait_recv()

    def queries(t):
        wait_rows(t)
        for h in range(2):
            prepare_queries(t, h)

    def values(t):
        for h in range(2):
            wait_arriving(t, h)
            prepare_arriving(t, h)
        values_pass(t)

    def gain_send(d):
        return remote(gacc, gr.at[d], g_s.at[d], g_r.at[d], {"ctx": ctx_peer(d)})

    def add_gain(d, total):
        gain_send(d).wait_recv()
        return total + gr[d]

    own_gain = pl.ds(pl.multiple_of(tp * group, group), group)

    def gain_share(d):
        return remote(
            gr.at[0], gain_out.at[own_gain, :], h_s.at[d], h_r.at[d], {"tp": tp_peer(d)}
        )

    for which in range(2):
        forward_kv(0, which)
    queries(0)
    softmax(0)
    for which in range(2):
        forward_kv(1, which)
    values(0)
    keys_pass(0)
    for h in range(2):
        couple(0, h)
    queries(1)
    for h in range(2):
        finish(0, h)
    for which in range(2):
        send_to_partner(0, which)
    softmax(1)
    values(1)
    send_to_partner(1, 1)
    for which in range(2):
        send_to_owners(0, which)
    keys_pass(1)
    send_to_partner(1, 0)
    for h in range(2):
        couple(1, h)

    @pl.loop(1, n)
    def _(d):
        gain_send(d).start()

    send_to_owners(1, 1)
    for h in range(2):
        finish(1, h)
    send_to_owners(1, 0)
    gain_total = lax.fori_loop(1, n, add_gain, gacc[...])
    gr[0] = gain_total
    own_gain_copy = pltpu.make_async_copy(gr.at[0], gain_out.at[own_gain, :], h_s.at[0])
    own_gain_copy.start()
    for d in range(1, n_tp):
        gain_share(d).start()

    def result_copy(t, which):
        out = (dk_out, dv_out)[which]
        return pltpu.make_async_copy(res.at[t, which], out.at[0, t], local_sem.at[t, which])

    for t in range(ticks):
        for which in (1, 0):
            partner_wait(t, which, line * high_first)
            for i, mine in enumerate((0, high_first)):
                middle = (n + 1 - me) // 2
                begin, end = (1, middle) if i == 0 else (middle, lines)
                from_partner = jnp.where(line == i, gp[t, mine, which].astype(f32), 0.0)

                def add(k, total, t=t, which=which):
                    owner_send(t, which, k).wait_recv()
                    return total + gz[t, k, which].astype(f32)

                res[t, which, half_rows(i), :] = lax.fori_loop(
                    begin, end, add, gf[t, mine, which] + from_partner
                )
            result_copy(t, which).start()

    for t in range(ticks):
        for d in range(1, n_tp):
            inv_send(t, d).wait_send()
            x_send(t, d).wait_send()
            if t == 0:
                a_send(t, d).wait_send()
            else:

                @pl.when(seg == last)
                def _(t=t, d=d):
                    a_send(t, d).wait_send()

            for h in range(2):
                coupling_send(t, h, d).wait_send()

        for which in range(2):
            for i in range(lines):
                kv_forward(t, which, i).wait_send()
                if i > 0:
                    kv_send(t, which, i).wait_send()
                    owner_send(t, which, i).wait_send()

            @pl.loop(0, lines)
            def _(i, t=t, which=which):
                partner_send(t, which, i).wait_send()

            result_copy(t, which).wait()

        if t + 1 < ticks:
            for h in range(2):

                @pl.when(seg > 0)
                def _(t=t, h=h):
                    pipe_send(t, h).wait_send()

        for j in range(n_tp):

            @pl.when(tp != j)
            def _(t=t, j=j):
                out_send(t, j).wait_send()

            @pl.when(tp == j)
            def _(t=t):
                out_own(t).wait()

        for d in range(1, n_tp):
            came = ig_out.at[0, t, :, own_cols]
            remote(came, came, o_s.at[t, d], o_r.at[t, d], {"tp": tp_peer(d)}).wait_recv()
    @pl.loop(1, n)
    def _(d):
        gain_send(d).wait_send()

    own_gain_copy.wait()

    for d in range(1, n_tp):
        gain_share(d).wait_send()
        gain_share(d).wait_recv()


def hand_over(*refs):
    *refs, sems = refs
    count = len(refs) // 3
    came, left, held = refs[:count], refs[count : 2 * count], refs[2 * count :]
    loads = [pltpu.make_async_copy(came[i], held[i], sems.at[0, i]) for i in range(count)]
    stores = [pltpu.make_async_copy(held[i], left[i], sems.at[1, i]) for i in range(count)]
    for c in loads:
        c.start()
    for load, store in zip(loads, stores):
        load.wait()
        store.start()
    for c in stores:
        c.wait()


def solution(mesh):
    n_pipe, n_ctx, n_tp = (mesh.shape[a] for a in ("pipe", "ctx", "tp"))

    def on_device(segment_inputs, keys, values, norm_gain, waiting_grads, output_grads, doc_lengths):
        ticks, rows, width = segment_inputs.shape[1:]
        cols = width // n_tp
        group = cols // HD
        docs = doc_lengths.shape[1]
        lanes = group * HALF
        slots = n_ctx + 2
        pairs = slots // 2
        dims = (n_pipe, n_ctx, n_tp, ticks, group, docs)
        dma = pltpu.SemaphoreType.DMA
        vmem = pltpu.VMEM
        hbm = pl.BlockSpec(memory_space=pl.ANY)
        lines = n_ctx // 2
        scratch = [
            vmem((ticks, rows, width), bf16),
            vmem((ticks, 2 * HALF, cols), bf16),
            vmem((ticks, 2 * HALF, cols), bf16),
            vmem((ticks, 2 * HALF, HD), f32),
            vmem((ticks, slots, 2, HALF, HD), bf16),
            vmem((ticks, 2, lanes, HD), bf16),
            vmem((2, lanes, HD), bf16),
            vmem((ticks, pairs, 2 * HALF, lanes), f32),
            vmem((pairs, 2 * HALF, lanes), f32),
            vmem((ticks, pairs, 1, lanes), f32),
            vmem((pairs, 1, lanes), f32),
            vmem((2, 1, lanes), f32),
            vmem((2, HD, lanes), f32),
            vmem((2, lanes, HD), bf16),
            vmem((ticks, slots, 2, HALF, HD), f32),
            vmem((ticks, slots, 2, HALF, HD), bf16),
            vmem((ticks, slots, 2, HALF, HD), bf16),
            vmem((ticks, lines, 2, HALF, HD), bf16),
            vmem((ticks, lines, 2, HALF, HD), bf16),
            vmem((ticks, 2 * HALF, cols), bf16),
            vmem((ticks, 2, 1, HD), f32),
            vmem((ticks, 2, n_tp, 1, HD), f32),
            vmem((group, HD), f32),
            vmem((n_ctx, group, HD), f32),
            vmem((ticks, 2, 2 * HALF, HD), f32),
            dma((ticks, 7)),
            dma((ticks, n_tp)),
            dma((ticks, n_tp)),
            dma((ticks, n_tp)),
            dma((ticks, n_tp)),
            dma((ticks, n_tp)),
            dma((ticks, n_tp)),
            dma((ticks, 2, lines)),
            dma((ticks, 2, slots)),
            dma((ticks, 2, lines)),
            dma((ticks, 2, lines)),
            dma((ticks, 2, slots)),
            dma((ticks, 2, lines)),
            dma((ticks, 2, lines)),
            dma((ticks, 2, n_tp)),
            dma((ticks, 2, n_tp)),
            dma((ticks, 2)),
            dma((ticks, 2)),
            dma((ticks, n_tp)),
            dma((ticks, n_tp)),
            dma((n_ctx,)),
            dma((n_ctx,)),
            dma((n_tp,)),
            dma((n_tp,)),
        ]
        on_chip = pl.BlockSpec(memory_space=pltpu.VMEM)
        input_grads, key_grads, value_grads, gain_grads = pl.pallas_call(
            functools.partial(kernel, dims),
            out_shape=(
                jax.ShapeDtypeStruct((1, ticks, rows, width), bf16),
                jax.ShapeDtypeStruct((1, ticks, 2 * HALF, HD), f32),
                jax.ShapeDtypeStruct((1, ticks, 2 * HALF, HD), f32),
                jax.ShapeDtypeStruct((width // HD, HD), f32),
            ),
            in_specs=[
                hbm,
                hbm,
                hbm,
                on_chip,
                hbm,
                hbm,
                pl.BlockSpec(memory_space=pltpu.SMEM),
            ],
            out_specs=(hbm,) * 4,
            scratch_shapes=scratch,
            compiler_params=pltpu.CompilerParams(
                collective_id=0, has_side_effects=True, vmem_limit_bytes=KERNEL_VMEM
            ),
            name="window",
        )(
            segment_inputs,
            keys,
            values,
            norm_gain.reshape(width // HD, HD),
            waiting_grads,
            output_grads,
            doc_lengths,
        )
        made = (input_grads, key_grads, value_grads, gain_grads)
        input_grads, key_grads, value_grads, gain_grads = pl.pallas_call(
            hand_over,
            out_shape=tuple(jax.ShapeDtypeStruct(a.shape, a.dtype) for a in made),
            in_specs=[hbm] * len(made),
            out_specs=(hbm,) * len(made),
            scratch_shapes=[vmem(a.shape, a.dtype) for a in made] + [dma((2, len(made)))],
            compiler_params=pltpu.CompilerParams(vmem_limit_bytes=KERNEL_VMEM),
            name="hand_over",
        )(*made)
        return input_grads, key_grads, value_grads, gain_grads.reshape(1, width)

    in_specs = (
        P("pipe", None, ("ctx", "tp"), None),
        P("pipe", None, "ctx", "tp"),
        P("pipe", None, "ctx", "tp"),
        P("pipe", None),
        P("pipe", ("ctx", "tp"), None),
        P(None, ("ctx", "tp"), None),
        P(),
    )
    out_specs = (
        P("pipe", None, ("ctx", "tp"), None),
        P("pipe", None, "ctx", "tp"),
        P("pipe", None, "ctx", "tp"),
        P("pipe", None),
    )
    return jax.shard_map(
        on_device, mesh=mesh, in_specs=in_specs, out_specs=out_specs, check_vma=False
    )
```

time: 79.7 us -> 61.9 us (0.78)
  Pallas kernels: 70 us -> 61 us
  local copies, waits for them, and re-layouts: 8.72 us -> 0 us
    pallas_call x1, Pallas kernels: 70 us -> 59 us  [on_device(): pl.pallas_call(functools.partial(kernel, dims), out_shape=(jax.ShapeDtype...]
    unnamed x18 -> x0, local copies, waits for them, and re-layouts: 8.72 us -> none
    pallas_call x0 -> x1, Pallas kernels: none -> 1.98 us  [on_device(): pl.pallas_call(hand_over, out_shape=tuple((jax.ShapeDtypeStruct(a.shape,...]
where the time goes in v2:
time: 61.9 us; the launch traced here: 61.6 us
  Pallas kernels  61 us (99%)
  between operations  0.64 us (1%)
    pallas_call x1, Pallas kernels, on_device(): pl.pallas_call(functools.partial(kernel, dims), out_shape=(jax.ShapeDtype...  59 us
    pallas_call x1, Pallas kernels, on_device(): pl.pallas_call(hand_over, out_shape=tuple((jax.ShapeDtypeStruct(a.shape,...  1.98 us

profile of v2, /device:TPU:1, one launch (start us, length us, event | category | flops | bytes accessed | tf_op | source)
XLA Modules:
  0.0 61.6 jit_solution(16242682520629311914)
XLA Ops:
  0.6 59.0 %window.1 = (bf16[1,2,32,4096]{3,2,1,0:T(8,128)(2,1)}, f32[1,2,128,128]{3,2,1,0:T(8,128)}, f32[1,2,128,128]{3,2,1,0:T(8,128)}, f32[32,128]{1,0:T(8,128)}) custom-call(bf16[1,2,32,4096]{3,2,1,0:T(8,128)(2,1)} %x_hbm.1, bf16[1,2,128,128]{3,2,1,0:T(8,128)(2,1)} %k_hbm.1, bf16[1,2,128,128]{3,2,1,0:T(8,128)(2,1)} %v_hbm.1, f32[32,128]{1,0:T(8,128)} %bitcast.2, ...), custom_call_target="tpu_custom_call" | custom-call | tf_op jit(solution)/shard_map/window/pallas_call | solution.py:821
  59.6 2.0 %hand_over.1 = (bf16[1,2,32,4096]{3,2,1,0:T(8,128)(2,1)}, f32[1,2,128,128]{3,2,1,0:T(8,128)}, f32[1,2,128,128]{3,2,1,0:T(8,128)}, f32[32,128]{1,0:T(8,128)}) custom-call(bf16[1,2,32,4096]{3,2,1,0:T(8,128)(2,1)} %get-tuple-element.12.refs_0_, f32[1,2,128,128]{3,2,1,0:T(8,128)} %get-tuple-element.13.refs_1_, f32[1,2,128,128]{3,2,1,0:T(8,128)} %get-tuple-element.14.refs_2_, ...), custom_call_target="tpu_custom_call" | custom-call | tf_op jit(solution)/shard_map/hand_over/pallas_call | solution.py:854

commit v3 on v2

--- a/solution.py
+++ b/solution.py
@@ -44,10 +44,10 @@
     x_hbm,
     k_hbm,
     v_hbm,
-    gain_ref,
+    gain_hbm,
     w_hbm,
     og_hbm,
-    doc_ref,
+    doc_hbm,
     ig_out,
     dk_out,
     dv_out,
@@ -77,7 +77,10 @@
     gacc,
     gr,
     res,
+    gain_ref,
+    doc_ref,
     local_sem,
+    small_sem,
     x_s,
     x_r,
     a_s,
@@ -141,12 +144,62 @@
     def partner_slot(slot, is_upper):
         return slot + (1 - 2 * line) * (1 - 2 * is_upper)
 
+    own_rows = pl.ds(pl.multiple_of(tp * rows, rows), rows)
+    own_cols = pl.ds(pl.multiple_of(tp * cols, cols), cols)
+
+    def kv_copies(t):
+        return [
+            pltpu.make_async_copy(
+                ref.at[0, t, pl.ds(i * HALF, HALF)], kv.at[t, slot, which], local_sem.at[t, 2 * which + i]
+            )
+            for which, ref in enumerate((k_hbm, v_hbm))
+            for i, slot in enumerate((0, high_first))
+        ]
+
+    def x_copy(t):
+        return pltpu.make_async_copy(x_hbm.at[0, t], xrow.at[t], local_sem.at[t, 4])
+
+    def own_x(t):
+        return pltpu.make_async_copy(
+            x_hbm.at[0, t, :, own_cols], xh.at[t, own_rows, :], local_sem.at[t, 5]
+        )
+
+    def own_a(t):
+        return pltpu.make_async_copy(
+            w_hbm.at[0, :, own_cols], ah.at[t, own_rows, :], local_sem.at[t, 6]
+        )
+
+    def own_output_grad(t):
+        return pltpu.make_async_copy(
+            og_hbm.at[t - 1, :, own_cols], ah.at[t, own_rows, :], local_sem.at[t, 6]
+        )
+
+    own_gain = pl.ds(pl.multiple_of(tp * group, group), group)
+    small_copies = (
+        pltpu.make_async_copy(gain_hbm.at[own_gain, :], gain_ref, small_sem.at[0]),
+        pltpu.make_async_copy(doc_hbm, doc_ref, small_sem.at[1]),
+    )
+    for t in range(ticks):
+        for c in kv_copies(t):
+            c.start()
+    for c in small_copies:
+        c.start()
+    for t in range(ticks):
+        x_copy(t).start()
+        own_x(t).start()
+        if t == 0:
+            own_a(t).start()
+        else:
+
+            @pl.when(seg == last)
+            def _(t=t):
+                own_output_grad(t).start()
+
     barrier = pltpu.get_barrier_semaphore()
 
-    @pl.loop(1, n)
-    def _(d):
-        pl.semaphore_signal(barrier, inc=1, device_id={"ctx": ctx_peer(d)}, device_id_type=MESH)
-
+    pl.semaphore_signal(barrier, inc=1, device_id={"ctx": partner}, device_id_type=MESH)
+    for i in far_first:
+        pl.semaphore_signal(barrier, inc=1, device_id={"ctx": ctx_peer(2 * i)}, device_id_type=MESH)
     for d in range(1, n_tp):
         pl.semaphore_signal(barrier, inc=1, device_id={"tp": tp_peer(d)}, device_id_type=MESH)
     pl.semaphore_signal(
@@ -156,50 +209,6 @@
         barrier, inc=1, device_id={"pipe": lax.rem(seg + n_pipe - 1, n_pipe)}, device_id_type=MESH
     )
 
-    own_rows = pl.ds(pl.multiple_of(tp * rows, rows), rows)
-    own_cols = pl.ds(pl.multiple_of(tp * cols, cols), cols)
-
-    def kv_copies(t):
-        return [
-            pltpu.make_async_copy(
-                ref.at[0, t, pl.ds(i * HALF, HALF)], kv.at[t, slot, which], local_sem.at[t, 2 * which + i]
-            )
-            for which, ref in enumerate((k_hbm, v_hbm))
-            for i, slot in enumerate((0, high_first))
-        ]
-
-    def x_copy(t):
-        return pltpu.make_async_copy(x_hbm.at[0, t], xrow.at[t], local_sem.at[t, 4])
-
-    def own_x(t):
-        return pltpu.make_async_copy(
-            x_hbm.at[0, t, :, own_cols], xh.at[t, own_rows, :], local_sem.at[t, 5]
-        )
-
-    def own_a(t):
-        return pltpu.make_async_copy(
-            w_hbm.at[0, :, own_cols], ah.at[t, own_rows, :], local_sem.at[t, 6]
-        )
-
-    def own_output_grad(t):
-        return pltpu.make_async_copy(
-            og_hbm.at[t - 1, :, own_cols], ah.at[t, own_rows, :], local_sem.at[t, 6]
-        )
-
-    for t in range(ticks):
-        for c in kv_copies(t):
-            c.start()
-    for t in range(ticks):
-        x_copy(t).start()
-        own_x(t).start()
-        if t == 0:
-            own_a(t).start()
-        else:
-
-            @pl.when(seg == last)
-            def _(t=t):
-                own_output_grad(t).start()
-
     odd = lax.rem(me, 2)
     pad_slot = (1 - odd) * (me + 1) + odd * (n + 1)
     for t in range(ticks):
@@ -208,7 +217,7 @@
         for c in kv_copies(t):
             c.wait()
 
-    pl.semaphore_wait(barrier, n - 1 + n_tp - 1 + 2)
+    pl.semaphore_wait(barrier, lines + n_tp - 1 + 2)
 
     def x_send(t, d):
         to = tp_peer(d)
@@ -303,7 +312,7 @@
                     a_send(t, d).start()
 
     def gain_of(g):
-        return gain_ref[pl.ds(tp * group + g, 1), :]
+        return gain_ref[g : g + 1, :]
 
     def half_rows(h):
         return slice(h * HALF, (h + 1) * HALF)
@@ -325,7 +334,7 @@
         for g in range(group):
             dos[h, head_rows(g), :] = ah[t, half_rows(h), head_cols(g)]
 
-    unroll = 3 if pairs % 3 == 0 else 1
+    unroll = pairs
 
     def each_group(step):
         @pl.loop(0, pairs // unroll)
@@ -601,22 +610,28 @@
             prepare_arriving(t, h)
         values_pass(t)
 
-    def gain_send(d):
-        return remote(gacc, gr.at[d], g_s.at[d], g_r.at[d], {"ctx": ctx_peer(d)})
-
-    def add_gain(d, total):
-        gain_send(d).wait_recv()
-        return total + gr[d]
-
-    own_gain = pl.ds(pl.multiple_of(tp * group, group), group)
+    def gain_send(i):
+        return remote(gacc, gr.at[i], g_s.at[i], g_r.at[i], {"ctx": ctx_peer(2 * i)})
+
+    def gain_of_line():
+        total = gacc[...]
+        for i in range(1, lines):
+            gain_send(i).wait_recv()
+            total = total + gr[i]
+        gr[0] = total
+        gain_across.start()
+
+    gain_across = remote(gr.at[0], gr.at[lines], g_s.at[0], g_r.at[0], {"ctx": partner})
 
     def gain_share(d):
         return remote(
-            gr.at[0], gain_out.at[own_gain, :], h_s.at[d], h_r.at[d], {"tp": tp_peer(d)}
+            gr.at[lines + 1], gain_out.at[own_gain, :], h_s.at[d], h_r.at[d], {"tp": tp_peer(d)}
         )
 
     for which in range(2):
         forward_kv(0, which)
+    for c in small_copies:
+        c.wait()
     queries(0)
     softmax(0)
     for which in range(2):
@@ -640,17 +655,18 @@
     for h in range(2):
         couple(1, h)
 
-    @pl.loop(1, n)
-    def _(d):
-        gain_send(d).start()
-
+    for i in far_first:
+        gain_send(i).start()
     send_to_owners(1, 1)
     for h in range(2):
         finish(1, h)
     send_to_owners(1, 0)
-    gain_total = lax.fori_loop(1, n, add_gain, gacc[...])
-    gr[0] = gain_total
-    own_gain_copy = pltpu.make_async_copy(gr.at[0], gain_out.at[own_gain, :], h_s.at[0])
+    gain_of_line()
+    gain_across.wait_recv()
+    gr[lines + 1] = gr[0] + gr[lines]
+    own_gain_copy = pltpu.make_async_copy(
+        gr.at[lines + 1], gain_out.at[own_gain, :], h_s.at[0]
+    )
     own_gain_copy.start()
     for d in range(1, n_tp):
         gain_share(d).start()
@@ -724,10 +740,9 @@
         for d in range(1, n_tp):
             came = ig_out.at[0, t, :, own_cols]
             remote(came, came, o_s.at[t, d], o_r.at[t, d], {"tp": tp_peer(d)}).wait_recv()
-    @pl.loop(1, n)
-    def _(d):
-        gain_send(d).wait_send()
-
+    for i in far_first:
+        gain_send(i).wait_send()
+    gain_across.wait_send()
     own_gain_copy.wait()
 
     for d in range(1, n_tp):
@@ -790,9 +805,12 @@
             vmem((ticks, 2, 1, HD), f32),
             vmem((ticks, 2, n_tp, 1, HD), f32),
             vmem((group, HD), f32),
-            vmem((n_ctx, group, HD), f32),
+            vmem((lines + 2, group, HD), f32),
             vmem((ticks, 2, 2 * HALF, HD), f32),
+            vmem((group, HD), f32),
+            pltpu.SMEM(doc_lengths.shape, jnp.int32),
             dma((ticks, 7)),
+            dma((2,)),
             dma((ticks, n_tp)),
             dma((ticks, n_tp)),
             dma((ticks, n_tp)),
@@ -812,12 +830,11 @@
             dma((ticks, 2)),
             dma((ticks, n_tp)),
             dma((ticks, n_tp)),
-            dma((n_ctx,)),
-            dma((n_ctx,)),
+            dma((lines,)),
+            dma((lines,)),
             dma((n_tp,)),
             dma((n_tp,)),
         ]
-        on_chip = pl.BlockSpec(memory_space=pltpu.VMEM)
         input_grads, key_grads, value_grads, gain_grads = pl.pallas_call(
             functools.partial(kernel, dims),
             out_shape=(
@@ -830,10 +847,10 @@
                 hbm,
                 hbm,
                 hbm,
-                on_chip,
                 hbm,
                 hbm,
-                pl.BlockSpec(memory_space=pltpu.SMEM),
+                hbm,
+                hbm,
             ],
             out_specs=(hbm,) * 4,
             scratch_shapes=scratch,

time: 61.9 us -> 58.8 us (0.950)
  Pallas kernels: 61 us -> 57.7 us
    pallas_call x1, Pallas kernels: 59 us -> 55.7 us  [on_device(): pl.pallas_call(functools.partial(kernel, dims), out_shape=(jax.ShapeDtype...]
where the time goes in v3:
time: 58.8 us; the launch traced here: 58.3 us
  Pallas kernels  57.7 us (98%)
  between operations  0.64 us (1%)
    pallas_call x1, Pallas kernels, on_device(): pl.pallas_call(functools.partial(kernel, dims), out_shape=(jax.ShapeDtype...  55.7 us
    pallas_call x1, Pallas kernels, on_device(): pl.pallas_call(hand_over, out_shape=tuple((jax.ShapeDtypeStruct(a.shape,...  1.98 us

profile of v3, /device:TPU:1, one launch (start us, length us, event | category | flops | bytes accessed | tf_op | source)
XLA Modules:
  0.0 58.3 jit_solution(4793490457320250539)
XLA Ops:
  0.6 55.7 %window.1 = (bf16[1,2,32,4096]{3,2,1,0:T(8,128)(2,1)}, f32[1,2,128,128]{3,2,1,0:T(8,128)}, f32[1,2,128,128]{3,2,1,0:T(8,128)}, f32[32,128]{1,0:T(8,128)}) custom-call(bf16[1,2,32,4096]{3,2,1,0:T(8,128)(2,1)} %x_hbm.1, bf16[1,2,128,128]{3,2,1,0:T(8,128)(2,1)} %k_hbm.1, bf16[1,2,128,128]{3,2,1,0:T(8,128)(2,1)} %v_hbm.1, f32[32,128]{1,0:T(8,128)} %bitcast.2, ...), custom_call_target="tpu_custom_call" | custom-call | tf_op jit(solution)/shard_map/window/pallas_call | solution.py:838
  56.4 2.0 %hand_over.1 = (bf16[1,2,32,4096]{3,2,1,0:T(8,128)(2,1)}, f32[1,2,128,128]{3,2,1,0:T(8,128)}, f32[1,2,128,128]{3,2,1,0:T(8,128)}, f32[32,128]{1,0:T(8,128)}) custom-call(bf16[1,2,32,4096]{3,2,1,0:T(8,128)(2,1)} %get-tuple-element.12.refs_0_, f32[1,2,128,128]{3,2,1,0:T(8,128)} %get-tuple-element.13.refs_1_, f32[1,2,128,128]{3,2,1,0:T(8,128)} %get-tuple-element.14.refs_2_, ...), custom_call_target="tpu_custom_call" | custom-call | tf_op jit(solution)/shard_map/hand_over/pallas_call | solution.py:871

commit v4 on v3

--- a/solution.py
+++ b/solution.py
@@ -640,16 +640,16 @@
     keys_pass(0)
     for h in range(2):
         couple(0, h)
+    for which in range(2):
+        send_to_partner(0, which)
     queries(1)
     for h in range(2):
         finish(0, h)
-    for which in range(2):
-        send_to_partner(0, which)
     softmax(1)
+    for which in (1, 0):
+        send_to_owners(0, which)
     values(1)
     send_to_partner(1, 1)
-    for which in range(2):
-        send_to_owners(0, which)
     keys_pass(1)
     send_to_partner(1, 0)
     for h in range(2):

time: 58.8 us -> 57.7 us (0.981)
  Pallas kernels: 57.7 us -> 56.9 us
    pallas_call x1, Pallas kernels: 55.7 us -> 54.9 us  [on_device(): pl.pallas_call(functools.partial(kernel, dims), out_shape=(jax.ShapeDtype...]
where the time goes in v4:
time: 57.7 us; the launch traced here: 57.5 us
  Pallas kernels  56.9 us (99%)
  between operations  0.64 us (1%)
    pallas_call x1, Pallas kernels, on_device(): pl.pallas_call(functools.partial(kernel, dims), out_shape=(jax.ShapeDtype...  54.9 us
    pallas_call x1, Pallas kernels, on_device(): pl.pallas_call(hand_over, out_shape=tuple((jax.ShapeDtypeStruct(a.shape,...  1.98 us

profile of v4, /device:TPU:1, one launch (start us, length us, event | category | flops | bytes accessed | tf_op | source)
XLA Modules:
  0.0 57.5 jit_solution(15192816734393340679)
XLA Ops:
  0.6 54.9 %window.1 = (bf16[1,2,32,4096]{3,2,1,0:T(8,128)(2,1)}, f32[1,2,128,128]{3,2,1,0:T(8,128)}, f32[1,2,128,128]{3,2,1,0:T(8,128)}, f32[32,128]{1,0:T(8,128)}) custom-call(bf16[1,2,32,4096]{3,2,1,0:T(8,128)(2,1)} %x_hbm.1, bf16[1,2,128,128]{3,2,1,0:T(8,128)(2,1)} %k_hbm.1, bf16[1,2,128,128]{3,2,1,0:T(8,128)(2,1)} %v_hbm.1, f32[32,128]{1,0:T(8,128)} %bitcast.2, ...), custom_call_target="tpu_custom_call" | custom-call | tf_op jit(solution)/shard_map/window/pallas_call | solution.py:838
  55.5 2.0 %hand_over.1 = (bf16[1,2,32,4096]{3,2,1,0:T(8,128)(2,1)}, f32[1,2,128,128]{3,2,1,0:T(8,128)}, f32[1,2,128,128]{3,2,1,0:T(8,128)}, f32[32,128]{1,0:T(8,128)}) custom-call(bf16[1,2,32,4096]{3,2,1,0:T(8,128)(2,1)} %get-tuple-element.12.refs_0_, f32[1,2,128,128]{3,2,1,0:T(8,128)} %get-tuple-element.13.refs_1_, f32[1,2,128,128]{3,2,1,0:T(8,128)} %get-tuple-element.14.refs_2_, ...), custom_call_target="tpu_custom_call" | custom-call | tf_op jit(solution)/shard_map/hand_over/pallas_call | solution.py:871

commit v5 on v4

--- a/solution.py
+++ b/solution.py
@@ -662,20 +662,22 @@
         finish(1, h)
     send_to_owners(1, 0)
     gain_of_line()
-    gain_across.wait_recv()
-    gr[lines + 1] = gr[0] + gr[lines]
-    own_gain_copy = pltpu.make_async_copy(
-        gr.at[lines + 1], gain_out.at[own_gain, :], h_s.at[0]
-    )
-    own_gain_copy.start()
-    for d in range(1, n_tp):
-        gain_share(d).start()
+    own_gain_copy = pltpu.make_async_copy(gr.at[lines + 1], gain_out.at[own_gain, :], h_s.at[0])
+
+    def share_gain():
+        gain_across.wait_recv()
+        gr[lines + 1] = gr[0] + gr[lines]
+        own_gain_copy.start()
+        for d in range(1, n_tp):
+            gain_share(d).start()
 
     def result_copy(t, which):
         out = (dk_out, dv_out)[which]
         return pltpu.make_async_copy(res.at[t, which], out.at[0, t], local_sem.at[t, which])
 
     for t in range(ticks):
+        if t == ticks - 1:
+            share_gain()
         for which in (1, 0):
             partner_wait(t, which, line * high_first)
             for i, mine in enumerate((0, high_first)):

time: 57.7 us -> 57.7 us (level)
  no operation moved by 1% of the time
where the time goes in v5:
time: 57.7 us; the launch traced here: 57.5 us
  Pallas kernels  56.9 us (99%)
  between operations  0.64 us (1%)
    pallas_call x1, Pallas kernels, on_device(): pl.pallas_call(functools.partial(kernel, dims), out_shape=(jax.ShapeDtype...  54.9 us
    pallas_call x1, Pallas kernels, on_device(): pl.pallas_call(hand_over, out_shape=tuple((jax.ShapeDtypeStruct(a.shape,...  1.98 us

profile of v5, /device:TPU:1, one launch (start us, length us, event | category | flops | bytes accessed | tf_op | source)
XLA Modules:
  0.0 57.5 jit_solution(5696298279951610740)
XLA Ops:
  0.6 54.9 %window.1 = (bf16[1,2,32,4096]{3,2,1,0:T(8,128)(2,1)}, f32[1,2,128,128]{3,2,1,0:T(8,128)}, f32[1,2,128,128]{3,2,1,0:T(8,128)}, f32[32,128]{1,0:T(8,128)}) custom-call(bf16[1,2,32,4096]{3,2,1,0:T(8,128)(2,1)} %x_hbm.1, bf16[1,2,128,128]{3,2,1,0:T(8,128)(2,1)} %k_hbm.1, bf16[1,2,128,128]{3,2,1,0:T(8,128)(2,1)} %v_hbm.1, f32[32,128]{1,0:T(8,128)} %bitcast.2, ...), custom_call_target="tpu_custom_call" | custom-call | tf_op jit(solution)/shard_map/window/pallas_call | solution.py:840
  55.5 2.0 %hand_over.1 = (bf16[1,2,32,4096]{3,2,1,0:T(8,128)(2,1)}, f32[1,2,128,128]{3,2,1,0:T(8,128)}, f32[1,2,128,128]{3,2,1,0:T(8,128)}, f32[32,128]{1,0:T(8,128)}) custom-call(bf16[1,2,32,4096]{3,2,1,0:T(8,128)(2,1)} %get-tuple-element.12.refs_0_, f32[1,2,128,128]{3,2,1,0:T(8,128)} %get-tuple-element.13.refs_1_, f32[1,2,128,128]{3,2,1,0:T(8,128)} %get-tuple-element.14.refs_2_, ...), custom_call_target="tpu_custom_call" | custom-call | tf_op jit(solution)/shard_map/hand_over/pallas_call | solution.py:873
